TPU v7x, 512 devices: a whole 4x8x8 slice. The times are simulated.
512 devices in a mesh: dp: 16 (over z, core), expert: 32 (over x, y).
Axes of the slice: x: 4, y: 8, z: 8, core: 2. Of those that a mesh axis runs over, the one named last changes fastest.
Arguments:
- pivot_states: bfloat16 [65536, 2048], P(('dp', 'expert')), may hold values from -6 to 6
- queries: bfloat16 [65536, 2048], P(('dp', 'expert')), may hold values from -8 to 8
- keys: bfloat16 [65536, 2048], P(('dp', 'expert')), may hold values from -8 to 8
- values: bfloat16 [65536, 2048], P(('dp', 'expert')), may hold values from -6 to 6
- pack_pos: int32 [65536], P(('dp', 'expert')), may hold values from 0 to 2047, as said below
- segment_ids: int32 [512, 128], P(('dp', 'expert')), may hold values from 0 to 7, never falling along the last dimension, each value on 1 to 64 neighbouring positions
- expert_ids: int32 [65536, 2], P(('dp', 'expert')), may hold values from 0 to 127, all different within a row
- gate_code: int32 [65536, 2], P(('dp', 'expert')), may hold values from 6554 to 65535
- ln_gain: float32 [2048], replicated, may hold values from 0.5 to 1.5
- ln_bias: float32 [2048], replicated, may hold values from -3 to 3
- w_in: bfloat16 [32, 2048, 4096], P('expert', None, 'dp'), may hold values from -0.125 to 0.125
- b_in: float32 [32, 4096], P('expert', 'dp'), may hold values from -3 to 3
- w_out: bfloat16 [32, 4096, 2048], P('expert', 'dp'), may hold values from -0.09375 to 0.09375
- b_out: float32 [32, 2048], replicated, may hold values from -3 to 3
Outputs:
- layer_out: bfloat16 [65536, 2048], P(('dp', 'expert'))
Inputs may be any that keep to these rules, and one draw needn't show every extreme that they name: Within one index of expert, pack_pos over the devices of dp is a permutation, and each device's tokens go exactly 8 to each packed block of its column. `expert_ids`: only ids below 32 belong to the experts of this round.
All inputs are finite; a program needn't handle non-finite values.
Results may differ from a plain program's by a relative error of at most 0.0055.
Values may be sent and summed in bfloat16 or wider, within the bound.
A program may use at most 64 MiB of HBM per device.

v0:
```python
import math

import jax
import jax.numpy as jnp
from jax import lax
from jax.sharding import PartitionSpec as P

HEAD_DIM = 128
ROUNDS = 4


epsilon = 1e-05
mask_fill = -1e30


def per_device(
    pivot_states,
    queries,
    keys,
    values,
    pack_pos,
    segment_ids,
    expert_ids,
    gate_code,
    ln_gain,
    ln_bias,
    w_in,
    b_in,
    w_out,
    b_out,
):
    tok_count = pivot_states.shape[0]
    model_width = pivot_states.shape[1]
    dp_count = lax.axis_size("dp")
    expert_count = lax.axis_size("expert")
    per_target = tok_count // dp_count
    target_block = pack_pos // tok_count
    offsets = pack_pos % tok_count
    target_hot = (target_block[:, None] == jnp.arange(dp_count, dtype=jnp.int32)[None, :]).astype(
        jnp.int32
    )
    bucket_rank = jnp.sum(jnp.cumsum(target_hot, axis=0) * target_hot, axis=1) - 1
    send_index = target_block * per_target + bucket_rank
    joined = jnp.concatenate([pivot_states, queries, keys, values], axis=1)
    send_rows = jnp.zeros_like(joined).at[send_index].set(joined)
    send_offsets = jnp.zeros_like(offsets).at[send_index].set(offsets)
    recv_rows, recv_offsets = (
        lax.all_to_all(send_rows, "dp", split_axis=0, concat_axis=0, tiled=True),
        lax.all_to_all(send_offsets, "dp", split_axis=0, concat_axis=0, tiled=True),
    )
    packed = jnp.zeros_like(recv_rows).at[recv_offsets].set(recv_rows)
    state_rows = packed[:, :model_width]
    query_rows = packed[:, model_width : 2 * model_width]
    key_rows = packed[:, 2 * model_width : 3 * model_width]
    value_rows = packed[:, 3 * model_width :]
    head_count = model_width // HEAD_DIM
    key_heads = key_rows.reshape(tok_count, head_count, HEAD_DIM)
    value_heads = value_rows.reshape(tok_count, head_count, HEAD_DIM)
    seg_row = segment_ids[0]
    block_rows = min(tok_count, 512)
    block_count = tok_count // block_rows
    score_scale = 1.0 / math.sqrt(HEAD_DIM)

    def attend(block_args):
        query_block, seg_block = block_args
        query_heads = query_block.reshape(block_rows, head_count, HEAD_DIM)
        scores = (
            jnp.einsum("qhd,khd->hqk", query_heads, key_heads, preferred_element_type=jnp.float32)
            * score_scale
        )
        same_doc = seg_block[:, None] == seg_row[None, :]
        scores = jnp.where(same_doc[None, :, :], scores, mask_fill)
        top_score = jnp.max(scores, axis=2, keepdims=True)
        exp_terms = jnp.exp(scores - top_score)
        softmax_weights = (exp_terms / jnp.sum(exp_terms, axis=2, keepdims=True)).astype(
            jnp.bfloat16
        )
        mixed_heads = jnp.einsum(
            "hqk,khd->qhd", softmax_weights, value_heads, preferred_element_type=jnp.float32
        )
        return mixed_heads.reshape(block_rows, model_width)

    attended = lax.map(
        attend,
        (
            query_rows.reshape(block_count, block_rows, model_width),
            seg_row.reshape(block_count, block_rows),
        ),
    )
    hidden_state = state_rows.astype(jnp.float32) + attended.reshape(tok_count, model_width)
    mean_value = jnp.mean(hidden_state, axis=1, keepdims=True)
    centered = hidden_state - mean_value
    variance = jnp.mean(centered * centered, axis=1, keepdims=True)
    normed = (centered * lax.rsqrt(variance + epsilon) * ln_gain + ln_bias).astype(jnp.bfloat16)
    capacity = max(2, 2 * tok_count // (ROUNDS * expert_count))
    assigned = jnp.concatenate([expert_ids[:, 0], expert_ids[:, 1]])
    expert_hot = (assigned[:, None] == jnp.arange(expert_count, dtype=jnp.int32)[None, :]).astype(
        jnp.int32
    )
    slot_rank = jnp.sum(jnp.cumsum(expert_hot, axis=0) * expert_hot, axis=1) - 1
    kept_mask = (assigned < expert_count) & (slot_rank < capacity)
    overflow = expert_count * capacity
    slot_index = jnp.where(kept_mask, assigned * capacity + slot_rank, overflow)
    buffer = jnp.zeros((overflow, model_width), jnp.bfloat16)
    buffer = (
        buffer.at[slot_index[:tok_count]]
        .set(normed, mode="drop")
        .at[slot_index[tok_count:]]
        .set(normed, mode="drop")
    )
    first_matrix = w_in[0]
    bias_in_row = b_in[0]
    second_matrix = w_out[0]
    arrived = lax.all_to_all(
        buffer.reshape(expert_count, capacity, model_width),
        "expert",
        split_axis=0,
        concat_axis=0,
        tiled=True,
    )
    arrived = arrived.reshape(overflow, model_width)
    hidden = jnp.dot(
        lax.all_gather(arrived, "dp", axis=0, tiled=True),
        first_matrix,
        preferred_element_type=jnp.float32,
    )
    hidden = jnp.maximum(hidden + bias_in_row, 0.0).astype(jnp.bfloat16)
    partial_value = jnp.dot(hidden, second_matrix, preferred_element_type=jnp.float32).astype(
        jnp.bfloat16
    )
    summed = lax.psum(partial_value, "dp").astype(jnp.float32)
    summed = lax.dynamic_slice_in_dim(summed, lax.axis_index("dp") * overflow, overflow, 0)
    bias_out_row = lax.dynamic_slice_in_dim(b_out, lax.axis_index("expert"), 1, 0)
    results = (summed + bias_out_row).astype(jnp.bfloat16)
    returned = lax.all_to_all(
        results.reshape(expert_count, capacity, model_width),
        "expert",
        split_axis=0,
        concat_axis=0,
        tiled=True,
    )
    returned = returned.reshape(overflow, model_width)
    gate_values = gate_code.astype(jnp.float32) / 65536.0
    gate_flat = jnp.concatenate([gate_values[:, 0], gate_values[:, 1]])
    weights = jnp.where(kept_mask, gate_flat, 0.0)
    guard_index = jnp.minimum(slot_index, overflow - 1)
    picked = returned[guard_index].astype(jnp.float32) * weights[:, None]
    layer_out = hidden_state + picked[:tok_count] + picked[tok_count:]
    return layer_out.astype(jnp.bfloat16)


def solution(mesh):
    return jax.shard_map(
        per_device,
        mesh=mesh,
        in_specs=(
            P(("dp", "expert"), None),
            P(("dp", "expert"), None),
            P(("dp", "expert"), None),
            P(("dp", "expert"), None),
            P(("dp", "expert")),
            P(("dp", "expert"), None),
            P(("dp", "expert"), None),
            P(("dp", "expert"), None),
            P(),
            P(),
            P("expert", None, "dp"),
            P("expert", "dp"),
            P("expert", "dp", None),
            P(),
        ),
        out_specs=P(("dp", "expert"), None),
        check_vma=False,
    )
```

profile of v0, /device:TPU:8, one launch (start us, length us, event | category | flops | bytes accessed | tf_op | source)
XLA Modules:
  0.0 335.2 jit_solution(7050097430861302124)
XLA Ops:
  6.5 0.8 and_select_fusion.1
  7.3 0.1 fusion.28
  7.4 0.2 reduce_window_sum.26
  7.6 0.2 select_reduce_fusion
  7.7 1.0 scatter_custom_fusion
  8.7 0.7 all_to_all.22
  9.4 10.4 %all-to-all-start = ((s32[16,8,1]{1,2,0:T(1,128)}), s32[16,8,1]{1,2,0:T(1,128)S(1)}, u32[]{:S(2)}, u32[]{:S(2)}) async-start(s32[16,8,1]{1,2,0:T(1,128)} %bitcast), calls=%async_computation | async-start | bytes 16384 | tf_op jit(solution)/shard_map/all_to_all | solution.py:49
  19.8 6.0 %scatter_custom_fusion.1 = bf16[128,8192]{1,0:T(8,128)(2,1)} fusion(s32[128]{0:T(128)S(1)} %compare_select_fusion.4, bf16[128,2048]{1,0:T(8,128)(2,1)} %param.17, bf16[]{:T(256)} %constant.122, bf16[128,2048]{1,0:T(8,128)(2,1)} %param.16, bf16[128,2048]{1,0:T(8,128)(2,1)} %param.15, bf16[128,2048]{1,0:T(8,128)(2,1)} %param.14, bf16[]{:T(256)} %constant.46.clone.1), kind=kCustom, calls=%fused_computation.8 | custom fusion | flops 8388608 | bytes 4194308 | tf_op jit(solution)/shard_map/scatter | solution.py:45
  25.8 1.6 all-to-all-done
  27.4 5.8 %all-to-all-start.1 = ((bf16[16,8,8192]{2,1,0:T(8,128)(2,1)}), bf16[16,8,8192]{2,1,0:T(8,128)(2,1)}, u32[]{:S(2)}, u32[]{:S(2)}) async-start(bf16[16,8,8192]{2,1,0:T(8,128)(2,1)} %bitcast.2), calls=%async_computation.1 | async-start | bytes 4194304 | tf_op jit(solution)/shard_map/all_to_all | solution.py:48
  33.3 0.6 reduce-window.6
  33.9 0.2 slice_reduce_fusion
  34.1 0.1 fusion.30
  34.3 0.1 broadcast_compare_fusion
  34.4 0.5 broadcast.249
  34.9 0.7 reduce.5
  35.6 0.1 all_to_all.24
  35.7 46.8 %all-to-all-done.1 = bf16[16,8,8192]{2,1,0:T(8,128)(2,1)} async-done(((bf16[16,8,8192]{2,1,0:T(8,128)(2,1)}), bf16[16,8,8192]{2,1,0:T(8,128)(2,1)}, u32[]{:S(2)}, u32[]{:S(2)}) %all-to-all-start.1) | async-done | bytes 2097184 | tf_op jit(solution)/shard_map/all_to_all | solution.py:48
  82.5 5.2 %scatter_custom_fusion.2 = bf16[128,8192]{1,0:T(8,128)(2,1)S(1)} fusion(s32[128]{0:T(128)S(1)} %fusion.32, bf16[16,8,8192]{2,1,0:T(8,128)(2,1)} %all-to-all-done.1, bf16[]{:T(256)} %constant.46.clone.1), kind=kCustom, calls=%fused_computation.16 | custom fusion | bytes 4194306 | tf_op jit(solution)/shard_map/scatter | solution.py:51
  87.7 1.3 fusion.39
  89.0 2.1 copy.28
  91.0 1.4 copy.29
  92.4 1.4 fusion.13
  93.8 0.2 fusion.41
  94.1 0.3 copy.27
  94.3 1.4 fusion.22
  95.8 1.6 copy.33
  97.3 1.2 fusion.38
  98.6 1.3 multiply_reduce_fusion
  99.9 1.3 add_convert_fusion
  101.2 1.4 scatter_custom_fusion.3
  102.6 1.5 scatter_fusion
  104.1 0.2 reshape.242
  104.3 22.6 %all_to_all.34 = bf16[32,2,2048]{2,1,0:T(2,128)(2,1)S(1)} all-to-all(bf16[32,2,2048]{2,1,0:T(2,128)(2,1)S(1)} %reshape.242), channel_id=1, replica_groups=mesh['dp'=16,'expert'=32] {'expert'}, dimensions={0} | all-to-all | bytes 524288 | tf_op jit(solution)/shard_map/all_to_all | solution.py:114
  126.9 0.8 reshape.243
  127.8 38.2 %all-gather.2.cloned.1.call-done = bf16[1024,2048]{1,0:T(8,128)(2,1)} async-done(((bf16[64,2048]{1,0:T(8,128)(2,1)}), bf16[1024,2048]{1,0:T(8,128)(2,1)}) %all-gather.2.cloned.1.call-update) | async-done | bytes 4194320 | tf_op jit(solution)/shard_map/all_gather | solution.py:123
  166.0 8.8 %convolution_convert_fusion = bf16[1024,2048]{1,0:T(8,128)(2,1)} fusion(bf16[1024,2048]{1,0:T(8,128)(2,1)} %all-gather.2.cloned.1.call-done, bf16[1,256,2048]{2,1,0:T(8,128)(2,1)S(1)} %copy-done, bf16[1,2048,256]{2,1,0:T(8,128)(2,1)} %param.24, f32[256]{0:T(256)S(1)} %bitcast.65), kind=kOutput, calls=%fused_computation.7 | convolution fusion | flops 2150367232 | bytes 10486784 | tf_op jit(solution)/shard_map/dot_general | solution.py:128
  174.8 0.6 copy-done.7
  175.5 0.9 constant_dynamic-slice_fusion
  176.3 124.8 %all-reduce.2.cloned.1.call-done = bf16[1024,2048]{1,0:T(8,128)(2,1)} async-done(((bf16[1024,2048]{1,0:T(8,128)(2,1)}), bf16[1024,2048]{1,0:T(8,128)(2,1)}) %all-reduce.2.cloned.1.call-update) | async-done | bytes 4194320 | tf_op jit(solution)/shard_map/psum | solution.py:131
  301.2 1.0 add_convert_fusion.1
  302.2 0.9 reshape.244
  303.0 9.8 %all-to-all-start.3 = ((bf16[32,2,2048]{2,1,0:T(2,128)(2,1)}), bf16[32,2,2048]{2,1,0:T(2,128)(2,1)S(1)}, u32[]{:S(2)}, u32[]{:S(2)}) async-start(bf16[32,2,2048]{2,1,0:T(2,128)(2,1)} %reshape.244), calls=%async_computation.3 | async-start | bytes 524288 | tf_op jit(solution)/shard_map/all_to_all | solution.py:135
  312.9 11.5 %all-to-all-done.3 = bf16[32,2,2048]{2,1,0:T(2,128)(2,1)S(1)} async-done(((bf16[32,2,2048]{2,1,0:T(2,128)(2,1)}), bf16[32,2,2048]{2,1,0:T(2,128)(2,1)S(1)}, u32[]{:S(2)}, u32[]{:S(2)}) %all-to-all-start.3) | async-done | bytes 262176 | tf_op jit(solution)/shard_map/all_to_all | solution.py:135
  324.5 0.1 reshape.245
  324.6 1.4 gather_fusion
  325.9 0.2 convert_multiply_fusion
  326.1 2.2 fusion.16
  (37 shorter events, 0.3 us)
Async XLA Ops:
  6.5 159.5 %copy-start = (bf16[1,256,2048]{2,1,0:T(8,128)(2,1)S(1)}, bf16[1,256,2048]{2,1,0:T(8,128)(2,1)}, u32[]{:S(2)}) copy-start(bf16[1,256,2048]{2,1,0:T(8,128)(2,1)} %param.26) | copy-start | bytes 3145732
  9.4 18.0 %all-to-all-start = ((s32[16,8,1]{1,2,0:T(1,128)}), s32[16,8,1]{1,2,0:T(1,128)S(1)}, u32[]{:S(2)}, u32[]{:S(2)}) async-start(s32[16,8,1]{1,2,0:T(1,128)} %bitcast), calls=%async_computation | async-start | bytes 16384 | tf_op jit(solution)/shard_map/all_to_all | solution.py:49
  27.4 5.9 %copy-start.6 = (s32[128,2]{0,1:T(2,128)S(1)}, s32[128,2]{0,1:T(2,128)}, u32[]{:S(2)}) copy-start(s32[128,2]{0,1:T(2,128)} %param.20) | copy-start | bytes 3076
  27.4 6.9 %copy-start.5 = (s32[1,128]{1,0:T(1,128)S(1)}, s32[1,128]{1,0:T(1,128)}, u32[]{:S(2)}) copy-start(s32[1,128]{1,0:T(1,128)} %param.19) | copy-start | bytes 1540
  27.4 55.1 %all-to-all-start.1 = ((bf16[16,8,8192]{2,1,0:T(8,128)(2,1)}), bf16[16,8,8192]{2,1,0:T(8,128)(2,1)}, u32[]{:S(2)}, u32[]{:S(2)}) async-start(bf16[16,8,8192]{2,1,0:T(8,128)(2,1)} %bitcast.2), calls=%async_computation.1 | async-start | bytes 4194304 | tf_op jit(solution)/shard_map/all_to_all | solution.py:48
  33.2 132.8 %all-gather.2.cloned.1.call-start = ((), (), s32[]{:S(2)}) async-start(), calls=%async_computation.4 | async-start | bytes 4456448 | tf_op jit(solution)/shard_map/all_gather | solution.py:123
  87.7 3.3 copy-start.1
  91.0 3.0 copy-start.2
  97.3 2.6 copy-start.3
  97.3 2.6 copy-start.4
  102.6 63.4 %copy-start.8 = (f32[1,256]{1,0:T(1,128)S(1)}, f32[1,256]{1,0:T(1,128)}, u32[]{:S(2)}) copy-start(f32[1,256]{1,0:T(1,128)} %param.25) | copy-start | bytes 3076
  127.8 173.4 %all-reduce.2.cloned.1.call-start = ((), (), s32[]{:S(2)}) async-start(), calls=%async_computation.5 | async-start | bytes 8388608 | tf_op jit(solution)/shard_map/psum | solution.py:131
  174.8 0.7 copy-start.7
  303.0 21.4 %all-to-all-start.3 = ((bf16[32,2,2048]{2,1,0:T(2,128)(2,1)}), bf16[32,2,2048]{2,1,0:T(2,128)(2,1)S(1)}, u32[]{:S(2)}, u32[]{:S(2)}) async-start(bf16[32,2,2048]{2,1,0:T(2,128)(2,1)} %reshape.244), calls=%async_computation.3 | async-start | bytes 524288 | tf_op jit(solution)/shard_map/all_to_all | solution.py:135
Sparse Core Ops, SparseCore 0:
  127.9 38.0 all-gather.1
  174.9 126.1 all-reduce.1
where the time goes:
time: 336 us; the launch traced here: 335 us
  waiting for transfers between devices  223 us (66%)
  starting transfers between devices  26.2 us (8%)
  blocking collectives  22.6 us (7%)
  local copies, waits for them, and re-layouts  21.9 us (7%)
  other arithmetic  16.2 us (5%)
  between operations  13.7 us (4%)
  matrix products  11.6 us (3%)
    psum x1, waiting for transfers between devices, per_device(): summed = lax.psum(partial_value, 'dp').astype(jnp.float32)  125 us
    all_to_all x1, waiting for transfers between devices, per_device(): lax.all_to_all(send_rows, 'dp', split_axis=0, concat_axis=0, tiled=True)  46.8 us
    all_gather x1, waiting for transfers between devices, per_device(): lax.all_gather(arrived, 'dp', axis=0, tiled=True)  38.2 us
    all_to_all x1, blocking collectives, per_device(): lax.all_to_all(buffer.reshape(expert_count, capacity, model_width), 'expe...  22.6 us
    all_to_all x1, waiting for transfers between devices, per_device(): lax.all_to_all(results.reshape(expert_count, capacity, model_width), 'exp...  11.5 us
    all_to_all x1, starting transfers between devices, per_device(): lax.all_to_all(send_offsets, 'dp', split_axis=0, concat_axis=0, tiled=True)  10.4 us
    all_to_all x1, starting transfers between devices, per_device(): lax.all_to_all(results.reshape(expert_count, capacity, model_width), 'exp...  9.85 us
    dot_general x1, matrix products, per_device(): jnp.dot(hidden, second_matrix, preferred_element_type=jnp.float32)  8.76 us
  transfers between devices with their start and end apart: 5, of which 5 were waited for; matrix products, arithmetic and copies ran while one was open for 3% of the time, Pallas kernels for 0%

commit v1 on v0

--- a/solution.py
+++ b/solution.py
@@ -3,6 +3,8 @@
 import jax
 import jax.numpy as jnp
 from jax import lax
+from jax.experimental import pallas as pl
+from jax.experimental.pallas import tpu as pltpu
 from jax.sharding import PartitionSpec as P
 
 HEAD_DIM = 128
@@ -11,6 +13,210 @@
 
 epsilon = 1e-05
 mask_fill = -1e30
+
+
+MESH_ID = pl.DeviceIdType.MESH
+
+
+def expert_kernel(
+    x_ref,
+    w1_ref,
+    b1_ref,
+    w2_ref,
+    b2_ref,
+    o_ref,
+    rows,
+    part,
+    pair_in,
+    run_out,
+    run_in,
+    w1_v,
+    w2_v,
+    load_sem,
+    ag_send,
+    ag_recv,
+    sib_send,
+    sib_recv,
+    pair_send,
+    pair_recv,
+    run_send,
+    run_recv,
+):
+    chips = lax.axis_size("dp") // 2
+    me = lax.axis_index("dp")
+    z = me // 2
+    core = me % 2
+    ahead = ((z + 1) % chips) * 2 + core
+    behind = ((z + chips - 1) % chips) * 2 + core
+    sibling = z * 2 + 1 - core
+    half, width = rows.shape[3], rows.shape[4]
+    steps = chips
+
+    loads = (
+        pltpu.make_async_copy(x_ref, rows.at[0, 0], load_sem.at[0]),
+        pltpu.make_async_copy(w1_ref.at[0], w1_v, load_sem.at[1]),
+        pltpu.make_async_copy(w2_ref.at[0], w2_v, load_sem.at[2]),
+    )
+    for load in loads:
+        load.start()
+    barrier = pltpu.get_barrier_semaphore()
+    for peer in (ahead, behind, sibling):
+        pl.semaphore_signal(barrier, inc=1, device_id={"dp": peer}, device_id_type=MESH_ID)
+    pl.semaphore_wait(barrier, 3)
+    loads[0].wait()
+
+    def pass_on(s, way):
+        return pltpu.make_async_remote_copy(
+            src_ref=rows.at[s, 0, way],
+            dst_ref=rows.at[s + 1, 0, way],
+            send_sem=ag_send.at[s, way],
+            recv_sem=ag_recv.at[s, way],
+            device_id={"dp": (ahead, behind)[way]},
+            device_id_type=MESH_ID,
+        )
+
+    def to_sibling(s):
+        return pltpu.make_async_remote_copy(
+            src_ref=rows.at[s, 0],
+            dst_ref=rows.at[s, 1],
+            send_sem=sib_send.at[s],
+            recv_sem=sib_recv.at[s],
+            device_id={"dp": sibling},
+            device_id_type=MESH_ID,
+        )
+
+    def pair(s):
+        return pltpu.make_async_remote_copy(
+            src_ref=part.at[s, 1],
+            dst_ref=pair_in.at[s],
+            send_sem=pair_send.at[s],
+            recv_sem=pair_recv.at[s],
+            device_id={"dp": sibling},
+            device_id_type=MESH_ID,
+        )
+
+    def run(s, way):
+        return pltpu.make_async_remote_copy(
+            src_ref=run_out.at[s - 1, way],
+            dst_ref=run_in.at[s - 1, way],
+            send_sem=run_send.at[s - 1, way],
+            recv_sem=run_recv.at[s - 1, way],
+            device_id={"dp": (ahead, behind)[way]},
+            device_id_type=MESH_ID,
+        )
+
+    def step(i, carry):
+        @pl.when(i < steps)
+        def _():
+            @pl.when(i >= 1)
+            def _():
+                for way in range(2):
+                    pass_on(i - 1, way).wait_recv()
+
+            @pl.when(i < steps - 1)
+            def _():
+                for way in range(2):
+                    pass_on(i, way).start()
+
+            to_sibling(i).start()
+
+        @pl.when(i == 1)
+        def _():
+            loads[1].wait()
+            loads[2].wait()
+
+        @pl.when((i >= 1) & (i <= steps))
+        def _():
+            s = i - 1
+            to_sibling(s).wait_recv()
+            held = rows[s].reshape(4 * half, width)
+            hidden = jnp.dot(held, w1_v[...], preferred_element_type=jnp.float32)
+            hidden = jnp.maximum(hidden + b1_ref[...], 0.0).astype(jnp.bfloat16)
+            share = jnp.dot(hidden, w2_v[...], preferred_element_type=jnp.float32)
+            part[s] = share.astype(jnp.bfloat16).reshape(2, 2, half, width)
+            pair(s).start()
+
+        @pl.when(i == 3)
+        def _():
+            pair(1).wait_recv()
+            total = part[1, 0].astype(jnp.float32) + pair_in[1].astype(jnp.float32)
+            run_out[0] = total.astype(jnp.bfloat16)
+            for way in range(2):
+                run(1, way).start()
+
+        @pl.when(i > 3)
+        def _():
+            s = i - 2
+            pair(s).wait_recv()
+            total = part[s, 0].astype(jnp.float32) + pair_in[s].astype(jnp.float32)
+            for way in range(2):
+                run(s - 1, way).wait_recv()
+            total = total + run_in[s - 2].astype(jnp.float32)
+            run_out[s - 1] = total.astype(jnp.bfloat16)
+            for way in range(2):
+                run(s, way).start()
+
+        return carry
+
+    lax.fori_loop(0, steps + 2, step, 0)
+    pair(0).wait_recv()
+    total = part[0, 0].astype(jnp.float32) + pair_in[0].astype(jnp.float32)
+    total = total + b2_ref[pl.ds(lax.axis_index("expert"), 1), :].reshape(1, 1, width)
+    for way in range(2):
+        run(steps - 1, way).wait_recv()
+    total = total + run_in[steps - 2].astype(jnp.float32)
+    o_ref[...] = total.astype(jnp.bfloat16).reshape(2 * half, width)
+
+    def drain(s, carry):
+        to_sibling(s).wait_send()
+        pair(s).wait_send()
+
+        @pl.when(s < steps - 1)
+        def _():
+            for way in range(2):
+                pass_on(s, way).wait_send()
+                run(s + 1, way).wait_send()
+
+        return carry
+
+    lax.fori_loop(0, steps, drain, 0)
+
+
+def experts(arrived, w_in, b_in, w_out, b_out):
+    count, width = arrived.shape
+    units = w_in.shape[2]
+    half = count // 2
+    chips = lax.axis_size("dp") // 2
+    dma = pltpu.SemaphoreType.DMA
+    bf16 = jnp.bfloat16
+    any_space = pl.BlockSpec(memory_space=pl.ANY)
+    vmem = pl.BlockSpec(memory_space=pltpu.VMEM)
+    return pl.pallas_call(
+        expert_kernel,
+        out_shape=jax.ShapeDtypeStruct((count, width), bf16),
+        in_specs=[any_space, any_space, vmem, any_space, vmem],
+        out_specs=vmem,
+        scratch_shapes=[
+            pltpu.VMEM((chips, 2, 2, half, width), bf16),
+            pltpu.VMEM((chips, 2, 2, half, width), bf16),
+            pltpu.VMEM((chips, 2, half, width), bf16),
+            pltpu.VMEM((chips - 1, 2, half, width), bf16),
+            pltpu.VMEM((chips - 1, 2, half, width), bf16),
+            pltpu.VMEM((width, units), bf16),
+            pltpu.VMEM((units, width), bf16),
+            dma((3,)),
+            dma((chips - 1, 2)),
+            dma((chips - 1, 2)),
+            dma((chips,)),
+            dma((chips,)),
+            dma((chips,)),
+            dma((chips,)),
+            dma((chips - 1, 2)),
+            dma((chips - 1, 2)),
+        ],
+        compiler_params=pltpu.CompilerParams(collective_id=1, has_side_effects=True),
+        name="expert_ring",
+    )(arrived.reshape(2, half, width), w_in, b_in, w_out, b_out)
 
 
 def per_device(
@@ -108,9 +314,6 @@
         .at[slot_index[tok_count:]]
         .set(normed, mode="drop")
     )
-    first_matrix = w_in[0]
-    bias_in_row = b_in[0]
-    second_matrix = w_out[0]
     arrived = lax.all_to_all(
         buffer.reshape(expert_count, capacity, model_width),
         "expert",
@@ -119,19 +322,7 @@
         tiled=True,
     )
     arrived = arrived.reshape(overflow, model_width)
-    hidden = jnp.dot(
-        lax.all_gather(arrived, "dp", axis=0, tiled=True),
-        first_matrix,
-        preferred_element_type=jnp.float32,
-    )
-    hidden = jnp.maximum(hidden + bias_in_row, 0.0).astype(jnp.bfloat16)
-    partial_value = jnp.dot(hidden, second_matrix, preferred_element_type=jnp.float32).astype(
-        jnp.bfloat16
-    )
-    summed = lax.psum(partial_value, "dp").astype(jnp.float32)
-    summed = lax.dynamic_slice_in_dim(summed, lax.axis_index("dp") * overflow, overflow, 0)
-    bias_out_row = lax.dynamic_slice_in_dim(b_out, lax.axis_index("expert"), 1, 0)
-    results = (summed + bias_out_row).astype(jnp.bfloat16)
+    results = experts(arrived, w_in, b_in, w_out, b_out)
     returned = lax.all_to_all(
         results.reshape(expert_count, capacity, model_width),
         "expert",

time: 336 us -> 205 us (0.61)
  waiting for transfers between devices: 223 us -> 72.1 us
  Pallas kernels: 0 us -> 57.7 us
  blocking collectives: 22.6 us -> 0 us
  between operations: 13.7 us -> 0.28 us
  matrix products: 11.6 us -> 4 us
  starting transfers between devices: 26.2 us -> 32 us
    psum x1 -> x0, waiting for transfers between devices: 125 us -> none  [per_device(): summed = lax.psum(partial_value, 'dp').astype(jnp.float32)]
    pallas_call x0 -> x1, Pallas kernels: none -> 57.7 us  [experts(): pl.pallas_call(expert_kernel, out_shape=jax.ShapeDtypeStruct((count, widt...]
    all_gather x1 -> x0, waiting for transfers between devices: 38.2 us -> none  [per_device(): lax.all_gather(arrived, 'dp', axis=0, tiled=True)]
    all_to_all x1 -> x0, blocking collectives: 22.6 us -> none  [per_device(): lax.all_to_all(buffer.reshape(expert_count, capacity, model_width), 'expe...]
    all_to_all x0 -> x1, waiting for transfers between devices: none -> 12.6 us  [per_device(): lax.all_to_all(buffer.reshape(expert_count, capacity, model_width), 'expe...]
    all_to_all x0 -> x1, starting transfers between devices: none -> 10.2 us  [per_device(): lax.all_to_all(buffer.reshape(expert_count, capacity, model_width), 'expe...]
    dot_general x1 -> x0, matrix products: 8.76 us -> none  [per_device(): jnp.dot(hidden, second_matrix, preferred_element_type=jnp.float32)]
    all_to_all x1, starting transfers between devices: 9.85 us -> 5.59 us  [per_device(): lax.all_to_all(results.reshape(expert_count, capacity, model_width), 'exp...]
  transfers between devices with their start and end apart: 5 -> 4, of which waited for: 5 -> 4; matrix products, arithmetic and copies ran while one was open for 3% -> 4% of each run, Pallas kernels for 0% -> 0%
where the time goes in v1:
time: 205 us; the launch traced here: 204 us
  waiting for transfers between devices  72.1 us (35%)
  Pallas kernels  57.7 us (28%)
  starting transfers between devices  32 us (16%)
  local copies, waits for them, and re-layouts  25.2 us (12%)
  other arithmetic  12.9 us (6%)
  matrix products  4 us (2%)
    pallas_call x1, Pallas kernels, experts(): pl.pallas_call(expert_kernel, out_shape=jax.ShapeDtypeStruct((count, widt...  57.7 us
    all_to_all x1, waiting for transfers between devices, per_device(): lax.all_to_all(send_rows, 'dp', split_axis=0, concat_axis=0, tiled=True)  46.9 us
    all_to_all x1, waiting for transfers between devices, per_device(): lax.all_to_all(buffer.reshape(expert_count, capacity, model_width), 'expe...  12.6 us
    all_to_all x1, waiting for transfers between devices, per_device(): lax.all_to_all(results.reshape(expert_count, capacity, model_width), 'exp...  11 us
    all_to_all x1, starting transfers between devices, per_device(): lax.all_to_all(send_offsets, 'dp', split_axis=0, concat_axis=0, tiled=True)  10.4 us
    all_to_all x1, starting transfers between devices, per_device(): lax.all_to_all(buffer.reshape(expert_count, capacity, model_width), 'expe...  10.2 us
    scatter x1, other arithmetic, per_device(): send_rows = jnp.zeros_like(joined).at[send_index].set(joined)  5.97 us
    all_to_all x1, starting transfers between devices, per_device(): lax.all_to_all(send_rows, 'dp', split_axis=0, concat_axis=0, tiled=True)  5.84 us
  transfers between devices with their start and end apart: 4, of which 4 were waited for; matrix products, arithmetic and copies ran while one was open for 4% of the time, Pallas kernels for 0%

profile of v1, /device:TPU:8, one launch (start us, length us, event | category | flops | bytes accessed | tf_op | source)
XLA Modules:
  0.0 204.3 jit_solution(10476686824540584588)
XLA Ops:
  0.0 0.7 and_select_fusion.1
  0.7 0.1 fusion.21
  0.8 0.2 reduce_window_sum.26
  0.9 0.2 select_reduce_fusion
  1.1 1.0 scatter_custom_fusion
  2.1 0.7 all_to_all.22
  2.8 10.4 %all-to-all-start = ((s32[16,8,1]{1,2,0:T(1,128)}), s32[16,8,1]{1,2,0:T(1,128)S(1)}, u32[]{:S(2)}, u32[]{:S(2)}) async-start(s32[16,8,1]{1,2,0:T(1,128)} %bitcast), calls=%async_computation | async-start | bytes 16384 | tf_op jit(solution)/shard_map/all_to_all | solution.py:255
  13.2 6.0 %scatter_custom_fusion.1 = bf16[128,8192]{1,0:T(8,128)(2,1)} fusion(s32[128]{0:T(128)S(1)} %compare_select_fusion.4, bf16[128,2048]{1,0:T(8,128)(2,1)} %param.17, bf16[]{:T(256)} %constant.109, bf16[128,2048]{1,0:T(8,128)(2,1)} %param.16, bf16[128,2048]{1,0:T(8,128)(2,1)} %param.15, bf16[128,2048]{1,0:T(8,128)(2,1)} %param.14, bf16[]{:T(256)} %constant.51.clone.1), kind=kCustom, calls=%fused_computation.7 | custom fusion | flops 8388608 | bytes 4194308 | tf_op jit(solution)/shard_map/scatter | solution.py:251
  19.2 1.6 all-to-all-done
  20.8 5.8 %all-to-all-start.1 = ((bf16[16,8,8192]{2,1,0:T(8,128)(2,1)}), bf16[16,8,8192]{2,1,0:T(8,128)(2,1)}, u32[]{:S(2)}, u32[]{:S(2)}) async-start(bf16[16,8,8192]{2,1,0:T(8,128)(2,1)} %bitcast.2), calls=%async_computation.1 | async-start | bytes 4194304 | tf_op jit(solution)/shard_map/all_to_all | solution.py:254
  26.7 0.6 reduce-window.6
  27.2 0.2 slice_reduce_fusion
  27.5 0.1 fusion.23
  27.6 0.1 broadcast_compare_fusion
  27.7 0.5 broadcast.249
  28.2 0.7 reduce.5
  28.9 0.1 all_to_all.24
  29.0 46.9 %all-to-all-done.1 = bf16[16,8,8192]{2,1,0:T(8,128)(2,1)} async-done(((bf16[16,8,8192]{2,1,0:T(8,128)(2,1)}), bf16[16,8,8192]{2,1,0:T(8,128)(2,1)}, u32[]{:S(2)}, u32[]{:S(2)}) %all-to-all-start.1) | async-done | bytes 2097184 | tf_op jit(solution)/shard_map/all_to_all | solution.py:254
  75.9 5.2 %scatter_custom_fusion.2 = bf16[128,8192]{1,0:T(8,128)(2,1)S(1)} fusion(s32[128]{0:T(128)S(1)} %fusion.25, bf16[16,8,8192]{2,1,0:T(8,128)(2,1)} %all-to-all-done.1, bf16[]{:T(256)} %constant.51.clone.1), kind=kCustom, calls=%fused_computation.15 | custom fusion | bytes 4194306 | tf_op jit(solution)/shard_map/scatter | solution.py:257
  81.1 0.9 fusion.31
  82.0 1.0 copy.29
  83.0 1.0 copy.28
  84.0 1.5 fusion.13
  85.6 0.2 fusion.33
  85.8 2.1 %copy.27 = bf16[128,2048]{0,1:T(8,128)(2,1)} copy(bf16[128,2048]{1,0:T(8,128)(2,1)} %get-tuple-element.17) | data formatting | bytes 1048576 | tf_op jit(solution)/shard_map/slice | solution.py:261
  87.9 2.5 %fusion.17 = f32[16,128,128]{2,1,0:T(8,128)} fusion(bf16[128,16,128]{0,2,1:T(8,128)(2,1)} %bitcast.55, f32[16,128]{1,0:T(8,128)S(1)} %fusion.33, f32[16,128,128]{1,2,0:T(8,128)S(1)} %fusion.13), kind=kOutput, calls=%fused_computation.31 | convolution fusion | flops 67897472 | bytes 2629632 | tf_op jit(solution)/shard_map/while/body/eval_jaxpr/hqk,khd->qhd/dot_general | solution.py:284
  90.3 1.6 copy.33
  91.9 0.0 copy-start
  91.9 0.2 fusion.30
  92.1 0.3 multiply_reduce_fusion
  92.4 0.2 copy-done
  92.6 0.0 copy-done.1
  92.6 1.1 add_convert_fusion
  93.7 1.9 scatter_custom_fusion.3
  95.6 0.0 copy-start.4
  95.6 2.0 scatter_fusion
  97.6 0.9 reshape.239
  98.5 10.2 %all-to-all-start.2 = ((bf16[32,2,2048]{2,1,0:T(2,128)(2,1)}), bf16[32,2,2048]{2,1,0:T(2,128)(2,1)S(1)}, u32[]{:S(2)}, u32[]{:S(2)}) async-start(bf16[32,2,2048]{2,1,0:T(2,128)(2,1)} %reshape.239), calls=%async_computation.2 | async-start | bytes 524288 | tf_op jit(solution)/shard_map/all_to_all | solution.py:317
  108.7 12.6 %all-to-all-done.2 = bf16[32,2,2048]{2,1,0:T(2,128)(2,1)S(1)} async-done(((bf16[32,2,2048]{2,1,0:T(2,128)(2,1)}), bf16[32,2,2048]{2,1,0:T(2,128)(2,1)S(1)}, u32[]{:S(2)}, u32[]{:S(2)}) %all-to-all-start.2) | async-done | bytes 262176 | tf_op jit(solution)/shard_map/all_to_all | solution.py:317
  121.3 0.8 reshape_reshape.3.x_ref
  122.1 57.7 %expert_ring.1 = bf16[64,2048]{1,0:T(8,128)(2,1)} custom-call(bf16[2,32,2048]{2,1,0:T(8,128)(2,1)} %reshape_reshape.3.x_ref, bf16[1,2048,256]{2,1,0:T(8,128)(2,1)} %w1_ref.1, f32[1,256]{1,0:T(1,128)} %b1_ref.1, bf16[1,256,2048]{2,1,0:T(8,128)(2,1)} %w2_ref.1, f32[32,2048]{1,0:T(8,128)} %b2_ref.1), custom_call_target="tpu_custom_call" | custom-call | tf_op jit(solution)/shard_map/expert_ring/pallas_call | solution.py:194
  179.8 1.8 reshape.240
  181.7 5.6 %all-to-all-start.3 = ((bf16[32,2,2048]{2,1,0:T(2,128)(2,1)}), bf16[32,2,2048]{2,1,0:T(2,128)(2,1)}, u32[]{:S(2)}, u32[]{:S(2)}) async-start(bf16[32,2,2048]{2,1,0:T(2,128)(2,1)} %reshape.240), calls=%async_computation.3 | async-start | bytes 524288 | tf_op jit(solution)/shard_map/all_to_all | solution.py:326
  187.3 11.0 %all-to-all-done.3 = bf16[32,2,2048]{2,1,0:T(2,128)(2,1)} async-done(((bf16[32,2,2048]{2,1,0:T(2,128)(2,1)}), bf16[32,2,2048]{2,1,0:T(2,128)(2,1)}, u32[]{:S(2)}, u32[]{:S(2)}) %all-to-all-start.3) | async-done | bytes 262176 | tf_op jit(solution)/shard_map/all_to_all | solution.py:326
  198.3 1.0 reshape.241
  199.4 2.3 %gather_fusion = bf16[256,2048]{1,0:T(8,128)(2,1)} fusion(bf16[64,2048]{1,0:T(8,128)(2,1)S(1)} %reshape.241, s32[1024]{0:T(1024)S(1)} %pad_clamp_fusion), kind=kCustom, calls=%fused_computation | custom fusion | bytes 2098176 | tf_op jit(solution)/shard_map/gather | solution.py:338
  201.7 1.4 convert_multiply_fusion
  203.1 1.1 fusion.14
  (22 shorter events, 0.2 us)
Async XLA Ops:
  2.8 18.0 %all-to-all-start = ((s32[16,8,1]{1,2,0:T(1,128)}), s32[16,8,1]{1,2,0:T(1,128)S(1)}, u32[]{:S(2)}, u32[]{:S(2)}) async-start(s32[16,8,1]{1,2,0:T(1,128)} %bitcast), calls=%async_computation | async-start | bytes 16384 | tf_op jit(solution)/shard_map/all_to_all | solution.py:255
  20.7 5.9 %copy-start.3 = (s32[128,2]{0,1:T(2,128)S(1)}, s32[128,2]{0,1:T(2,128)}, u32[]{:S(2)}) copy-start(s32[128,2]{0,1:T(2,128)} %param.20) | copy-start | bytes 3076
  20.8 6.9 %copy-start.2 = (s32[1,128]{1,0:T(1,128)S(1)}, s32[1,128]{1,0:T(1,128)}, u32[]{:S(2)}) copy-start(s32[1,128]{1,0:T(1,128)} %param.19) | copy-start | bytes 1540
  20.8 55.1 %all-to-all-start.1 = ((bf16[16,8,8192]{2,1,0:T(8,128)(2,1)}), bf16[16,8,8192]{2,1,0:T(8,128)(2,1)}, u32[]{:S(2)}, u32[]{:S(2)}) async-start(bf16[16,8,8192]{2,1,0:T(8,128)(2,1)} %bitcast.2), calls=%async_computation.1 | async-start | bytes 4194304 | tf_op jit(solution)/shard_map/all_to_all | solution.py:254
  91.9 0.7 copy-start
  91.9 0.7 copy-start.1
  95.6 13.1 %copy-start.4 = (s32[128,2]{0,1:T(2,128)S(1)}, s32[128,2]{0,1:T(2,128)}, u32[]{:S(2)}) copy-start(s32[128,2]{0,1:T(2,128)} %param.21) | copy-start | bytes 3076
  98.5 22.8 %all-to-all-start.2 = ((bf16[32,2,2048]{2,1,0:T(2,128)(2,1)}), bf16[32,2,2048]{2,1,0:T(2,128)(2,1)S(1)}, u32[]{:S(2)}, u32[]{:S(2)}) async-start(bf16[32,2,2048]{2,1,0:T(2,128)(2,1)} %reshape.239), calls=%async_computation.2 | async-start | bytes 524288 | tf_op jit(solution)/shard_map/all_to_all | solution.py:317
  181.7 16.6 %all-to-all-start.3 = ((bf16[32,2,2048]{2,1,0:T(2,128)(2,1)}), bf16[32,2,2048]{2,1,0:T(2,128)(2,1)}, u32[]{:S(2)}, u32[]{:S(2)}) async-start(bf16[32,2,2048]{2,1,0:T(2,128)(2,1)} %reshape.240), calls=%async_computation.3 | async-start | bytes 524288 | tf_op jit(solution)/shard_map/all_to_all | solution.py:326

commit v2 on v1

--- a/solution.py
+++ b/solution.py
@@ -8,7 +8,7 @@
 from jax.sharding import PartitionSpec as P
 
 HEAD_DIM = 128
-ROUNDS = 4
+CAP = 2
 
 
 epsilon = 1e-05
@@ -219,6 +219,337 @@
     )(arrived.reshape(2, half, width), w_in, b_in, w_out, b_out)
 
 
+F32 = jnp.float32
+BF16 = jnp.bfloat16
+
+
+def iota(shape, axis):
+    return lax.broadcasted_iota(jnp.int32, shape, axis)
+
+
+def as_column(row):
+    count = row.shape[1]
+    return jnp.transpose(jnp.broadcast_to(row, (count, count)))
+
+
+def earlier_equal(row):
+    count = row.shape[1]
+    same = as_column(row) == jnp.broadcast_to(row, (count, count))
+    before = iota((count, count), 0) < iota((count, count), 1)
+    return jnp.sum((same & before).astype(F32), axis=0, keepdims=True)
+
+
+def slot_row(ids_ref, expert_count):
+    ids = ids_ref[...].astype(F32)
+    assigned = jnp.concatenate([ids[0:1, :], ids[1:2, :]], axis=1)
+    rank = earlier_equal(assigned)
+    kept = (assigned < expert_count) & (rank < CAP)
+    return jnp.where(kept, assigned * CAP + rank, -1.0)
+
+
+def regroup_kernel(
+    pos_ref,
+    seg_ref,
+    ids_ref,
+    gain_ref,
+    bias_ref,
+    state_ref,
+    query_ref,
+    key_ref,
+    value_ref,
+    hidden_ref,
+    buffer_ref,
+    out_rows,
+    in_rows,
+    out_offs,
+    in_offs,
+    send_sem,
+    recv_sem,
+):
+    peers = lax.axis_size("dp")
+    experts_here = lax.axis_size("expert")
+    me = lax.axis_index("dp")
+    tokens, width = state_ref.shape
+    per_target = tokens // peers
+    chunks = out_rows.shape[0]
+    part = width // chunks
+    both = 2 * tokens
+
+    barrier = pltpu.get_barrier_semaphore()
+
+    def greet(k, carry):
+        pl.semaphore_signal(
+            barrier, inc=1, device_id={"dp": (me + k) % peers}, device_id_type=MESH_ID
+        )
+        return carry
+
+    lax.fori_loop(1, peers, greet, 0)
+
+    pos = pos_ref[...]
+    target = (pos // tokens).astype(F32)
+    offset = (pos % tokens).astype(F32)
+    place = target * (2 * per_target) + earlier_equal(target)
+    places = jnp.concatenate([place, place + per_target], axis=1).astype(jnp.int32)
+    spread = (iota((both, both), 0) == places).astype(F32).astype(BF16)
+    offset_column = as_column(offset)
+    offset_both = jnp.concatenate([offset_column, offset_column + tokens], axis=0).astype(BF16)
+    out_offs[...] = (
+        jnp.dot(spread, offset_both, preferred_element_type=F32)
+        .astype(BF16)
+        .reshape(peers, 2 * per_target, tokens)
+    )
+
+    def fill(c):
+        cols = pl.ds(pl.multiple_of(c * part, part), part)
+        upper = jnp.concatenate([state_ref[:, cols], query_ref[:, cols]], axis=1)
+        lower = jnp.concatenate([key_ref[:, cols], value_ref[:, cols]], axis=1)
+        joined = jnp.concatenate([upper, lower], axis=0)
+        out_rows[c] = (
+            jnp.dot(spread, joined, preferred_element_type=F32)
+            .astype(BF16)
+            .reshape(peers, 2 * per_target, 2 * part)
+        )
+
+    def send_rows(c, to, frm):
+        return pltpu.make_async_remote_copy(
+            src_ref=out_rows.at[c, to],
+            dst_ref=in_rows.at[c, frm],
+            send_sem=send_sem.at[c, to],
+            recv_sem=recv_sem.at[c, frm],
+            device_id={"dp": to},
+            device_id_type=MESH_ID,
+        )
+
+    def send_offs(to, frm):
+        return pltpu.make_async_remote_copy(
+            src_ref=out_offs.at[to],
+            dst_ref=in_offs.at[frm],
+            send_sem=send_sem.at[chunks, to],
+            recv_sem=recv_sem.at[chunks, frm],
+            device_id={"dp": to},
+            device_id_type=MESH_ID,
+        )
+
+    def own_rows(c):
+        return pltpu.make_async_copy(out_rows.at[c, me], in_rows.at[c, me], recv_sem.at[c, me])
+
+    own_offs = pltpu.make_async_copy(out_offs.at[me], in_offs.at[me], recv_sem.at[chunks, me])
+
+    def order(k):
+        step = (k + 1) // 2
+        return (me + peers + step * (2 * (k % 2) - 1)) % peers
+
+    fill(0)
+    pl.semaphore_wait(barrier, peers - 1)
+    own_offs.start()
+
+    def start_offs(k, carry):
+        send_offs(order(k), me).start()
+        return carry
+
+    lax.fori_loop(1, peers, start_offs, 0)
+
+    def start_chunk(c, carry):
+        @pl.when(c > 0)
+        def _():
+            fill(c)
+
+        own_rows(c).start()
+
+        def start_rows(k, inner):
+            send_rows(c, order(k), me).start()
+            return inner
+
+        return lax.fori_loop(1, peers, start_rows, carry)
+
+    lax.fori_loop(0, chunks, start_chunk, 0)
+
+    slots = slot_row(ids_ref, experts_here)
+    slot_hot = (iota((experts_here * CAP, both), 0) == slots.astype(jnp.int32)).astype(F32)
+    slot_hot = (slot_hot[:, :tokens] + slot_hot[:, tokens:]).astype(BF16)
+    segs = seg_ref[...].astype(F32)
+    same_doc = as_column(segs) == jnp.broadcast_to(segs, (tokens, tokens))
+
+    own_offs.wait()
+
+    def await_offs(k, carry):
+        send_offs(me, (me + k) % peers).wait_recv()
+        return carry
+
+    lax.fori_loop(1, peers, await_offs, 0)
+    offs = in_offs[...].reshape(both, tokens).astype(F32)
+    lanes = iota((both, tokens), 1).astype(F32)
+    gather = jnp.concatenate([offs == lanes, offs == lanes + tokens], axis=1).astype(F32)
+    gather = jnp.transpose(gather).astype(BF16)
+    score_scale = 1.0 / math.sqrt(HEAD_DIM)
+
+    def attend(c, carry):
+        own_rows(c).wait()
+
+        def await_rows(k, inner):
+            send_rows(c, me, (me + k) % peers).wait_recv()
+            return inner
+
+        lax.fori_loop(1, peers, await_rows, 0)
+        packed = jnp.dot(
+            gather, in_rows[c].reshape(both, 2 * part), preferred_element_type=F32
+        )
+        states = packed[:tokens, :part]
+        query = packed[:tokens, part:].astype(BF16)
+        key = packed[tokens:, :part].astype(BF16)
+        value = packed[tokens:, part:].astype(BF16)
+        for h in range(part // HEAD_DIM):
+            cols = slice(h * HEAD_DIM, (h + 1) * HEAD_DIM)
+            scores = lax.dot_general(
+                query[:, cols],
+                key[:, cols],
+                (((1,), (1,)), ((), ())),
+                preferred_element_type=F32,
+            )
+            scores = jnp.where(same_doc, scores * score_scale, mask_fill)
+            terms = jnp.exp(scores - jnp.max(scores, axis=1, keepdims=True))
+            probs = (terms / jnp.sum(terms, axis=1, keepdims=True)).astype(BF16)
+            mixed = jnp.dot(probs, value[:, cols], preferred_element_type=F32)
+            at = pl.ds(pl.multiple_of(c * part + h * HEAD_DIM, HEAD_DIM), HEAD_DIM)
+            hidden_ref[:, at] = states[:, cols] + mixed
+        return carry
+
+    lax.fori_loop(0, chunks, attend, 0)
+    hidden = hidden_ref[...]
+    centered = hidden - jnp.mean(hidden, axis=1, keepdims=True)
+    variance = jnp.mean(centered * centered, axis=1, keepdims=True)
+    normed = centered * lax.rsqrt(variance + epsilon) * gain_ref[...] + bias_ref[...]
+    buffer_ref[...] = jnp.dot(
+        slot_hot, normed.astype(BF16), preferred_element_type=F32
+    ).astype(BF16)
+
+    def drain(k, carry):
+        peer = (me + k) % peers
+        send_offs(peer, me).wait_send()
+
+        def drain_chunk(c, inner):
+            send_rows(c, peer, me).wait_send()
+            return inner
+
+        return lax.fori_loop(0, chunks, drain_chunk, carry)
+
+    lax.fori_loop(1, peers, drain, 0)
+
+
+def regroup_attend(states, queries, keys, values, pos, segs, ids, gain, bias):
+    tokens, width = states.shape
+    peers = lax.axis_size("dp")
+    slots = lax.axis_size("expert") * CAP
+    chunks = 4
+    group = 2 * tokens // peers
+    dma = pltpu.SemaphoreType.DMA
+    vmem = pl.BlockSpec(memory_space=pltpu.VMEM)
+    return pl.pallas_call(
+        regroup_kernel,
+        out_shape=(
+            jax.ShapeDtypeStruct((tokens, width), F32),
+            jax.ShapeDtypeStruct((slots, width), BF16),
+        ),
+        in_specs=[vmem] * 9,
+        out_specs=(vmem, vmem),
+        scratch_shapes=[
+            pltpu.VMEM((chunks, peers, group, 2 * width // chunks), BF16),
+            pltpu.VMEM((chunks, peers, group, 2 * width // chunks), BF16),
+            pltpu.VMEM((peers, group, tokens), BF16),
+            pltpu.VMEM((peers, group, tokens), BF16),
+            dma((chunks + 1, peers)),
+            dma((chunks + 1, peers)),
+        ],
+        compiler_params=pltpu.CompilerParams(collective_id=2, has_side_effects=True),
+        name="regroup_attend",
+    )(pos, segs, ids, gain, bias, states, queries, keys, values)
+
+
+def exchange_kernel(x_ref, o_ref, send_sem, recv_sem):
+    peers = lax.axis_size("expert")
+    me = lax.axis_index("expert")
+    barrier = pltpu.get_barrier_semaphore()
+
+    def greet(k, carry):
+        pl.semaphore_signal(
+            barrier, inc=1, device_id={"expert": (me + k) % peers}, device_id_type=MESH_ID
+        )
+        return carry
+
+    lax.fori_loop(1, peers, greet, 0)
+    own = pltpu.make_async_copy(x_ref.at[me], o_ref.at[me], recv_sem.at[me])
+    own.start()
+    pl.semaphore_wait(barrier, peers - 1)
+
+    def move(to, frm):
+        return pltpu.make_async_remote_copy(
+            src_ref=x_ref.at[to],
+            dst_ref=o_ref.at[frm],
+            send_sem=send_sem.at[to],
+            recv_sem=recv_sem.at[frm],
+            device_id={"expert": to},
+            device_id_type=MESH_ID,
+        )
+
+    def start(k, carry):
+        move((me + k) % peers, me).start()
+        return carry
+
+    lax.fori_loop(1, peers, start, 0)
+    own.wait()
+
+    def finish(k, carry):
+        peer = (me + k) % peers
+        move(me, peer).wait_recv()
+        move(peer, me).wait_send()
+        return carry
+
+    lax.fori_loop(1, peers, finish, 0)
+
+
+def exchange(rows, call_id):
+    peers = lax.axis_size("expert")
+    count, width = rows.shape
+    shape = (peers, count // peers, width)
+    dma = pltpu.SemaphoreType.DMA
+    vmem = pl.BlockSpec(memory_space=pltpu.VMEM)
+    moved = pl.pallas_call(
+        exchange_kernel,
+        out_shape=jax.ShapeDtypeStruct(shape, rows.dtype),
+        in_specs=[vmem],
+        out_specs=vmem,
+        scratch_shapes=[dma((peers,)), dma((peers,))],
+        compiler_params=pltpu.CompilerParams(collective_id=call_id, has_side_effects=True),
+        name="exchange",
+    )(rows.reshape(shape))
+    return moved.reshape(count, width)
+
+
+def combine_kernel(hidden_ref, ids_ref, gate_ref, rows_ref, o_ref):
+    tokens = hidden_ref.shape[0]
+    count = rows_ref.shape[0]
+    slots = slot_row(ids_ref, count // CAP)
+    total = hidden_ref[...]
+    gates = gate_ref[...].astype(F32) / 65536.0
+    for choice in range(2):
+        column = as_column(slots[:, choice * tokens : (choice + 1) * tokens])
+        hot = (column == iota((tokens, tokens), 1).astype(F32)).astype(F32).astype(BF16)
+        picked = jnp.dot(hot[:, :count], rows_ref[...], preferred_element_type=F32)
+        total = total + picked * gates[:, choice : choice + 1]
+    o_ref[...] = total.astype(BF16)
+
+
+def combine(hidden, ids, gate_code, rows):
+    vmem = pl.BlockSpec(memory_space=pltpu.VMEM)
+    return pl.pallas_call(
+        combine_kernel,
+        out_shape=jax.ShapeDtypeStruct(hidden.shape, BF16),
+        in_specs=[vmem] * 4,
+        out_specs=vmem,
+        name="combine",
+    )(hidden, ids, gate_code, rows)
+
+
 def per_device(
     pivot_states,
     queries,
@@ -235,109 +566,22 @@
     w_out,
     b_out,
 ):
-    tok_count = pivot_states.shape[0]
-    model_width = pivot_states.shape[1]
-    dp_count = lax.axis_size("dp")
-    expert_count = lax.axis_size("expert")
-    per_target = tok_count // dp_count
-    target_block = pack_pos // tok_count
-    offsets = pack_pos % tok_count
-    target_hot = (target_block[:, None] == jnp.arange(dp_count, dtype=jnp.int32)[None, :]).astype(
-        jnp.int32
+    ids = expert_ids.T
+    hidden_state, buffer = regroup_attend(
+        pivot_states,
+        queries,
+        keys,
+        values,
+        pack_pos[None, :],
+        segment_ids,
+        ids,
+        ln_gain[None, :],
+        ln_bias[None, :],
     )
-    bucket_rank = jnp.sum(jnp.cumsum(target_hot, axis=0) * target_hot, axis=1) - 1
-    send_index = target_block * per_target + bucket_rank
-    joined = jnp.concatenate([pivot_states, queries, keys, values], axis=1)
-    send_rows = jnp.zeros_like(joined).at[send_index].set(joined)
-    send_offsets = jnp.zeros_like(offsets).at[send_index].set(offsets)
-    recv_rows, recv_offsets = (
-        lax.all_to_all(send_rows, "dp", split_axis=0, concat_axis=0, tiled=True),
-        lax.all_to_all(send_offsets, "dp", split_axis=0, concat_axis=0, tiled=True),
-    )
-    packed = jnp.zeros_like(recv_rows).at[recv_offsets].set(recv_rows)
-    state_rows = packed[:, :model_width]
-    query_rows = packed[:, model_width : 2 * model_width]
-    key_rows = packed[:, 2 * model_width : 3 * model_width]
-    value_rows = packed[:, 3 * model_width :]
-    head_count = model_width // HEAD_DIM
-    key_heads = key_rows.reshape(tok_count, head_count, HEAD_DIM)
-    value_heads = value_rows.reshape(tok_count, head_count, HEAD_DIM)
-    seg_row = segment_ids[0]
-    block_rows = min(tok_count, 512)
-    block_count = tok_count // block_rows
-    score_scale = 1.0 / math.sqrt(HEAD_DIM)
-
-    def attend(block_args):
-        query_block, seg_block = block_args
-        query_heads = query_block.reshape(block_rows, head_count, HEAD_DIM)
-        scores = (
-            jnp.einsum("qhd,khd->hqk", query_heads, key_heads, preferred_element_type=jnp.float32)
-            * score_scale
-        )
-        same_doc = seg_block[:, None] == seg_row[None, :]
-        scores = jnp.where(same_doc[None, :, :], scores, mask_fill)
-        top_score = jnp.max(scores, axis=2, keepdims=True)
-        exp_terms = jnp.exp(scores - top_score)
-        softmax_weights = (exp_terms / jnp.sum(exp_terms, axis=2, keepdims=True)).astype(
-            jnp.bfloat16
-        )
-        mixed_heads = jnp.einsum(
-            "hqk,khd->qhd", softmax_weights, value_heads, preferred_element_type=jnp.float32
-        )
-        return mixed_heads.reshape(block_rows, model_width)
-
-    attended = lax.map(
-        attend,
-        (
-            query_rows.reshape(block_count, block_rows, model_width),
-            seg_row.reshape(block_count, block_rows),
-        ),
-    )
-    hidden_state = state_rows.astype(jnp.float32) + attended.reshape(tok_count, model_width)
-    mean_value = jnp.mean(hidden_state, axis=1, keepdims=True)
-    centered = hidden_state - mean_value
-    variance = jnp.mean(centered * centered, axis=1, keepdims=True)
-    normed = (centered * lax.rsqrt(variance + epsilon) * ln_gain + ln_bias).astype(jnp.bfloat16)
-    capacity = max(2, 2 * tok_count // (ROUNDS * expert_count))
-    assigned = jnp.concatenate([expert_ids[:, 0], expert_ids[:, 1]])
-    expert_hot = (assigned[:, None] == jnp.arange(expert_count, dtype=jnp.int32)[None, :]).astype(
-        jnp.int32
-    )
-    slot_rank = jnp.sum(jnp.cumsum(expert_hot, axis=0) * expert_hot, axis=1) - 1
-    kept_mask = (assigned < expert_count) & (slot_rank < capacity)
-    overflow = expert_count * capacity
-    slot_index = jnp.where(kept_mask, assigned * capacity + slot_rank, overflow)
-    buffer = jnp.zeros((overflow, model_width), jnp.bfloat16)
-    buffer = (
-        buffer.at[slot_index[:tok_count]]
-        .set(normed, mode="drop")
-        .at[slot_index[tok_count:]]
-        .set(normed, mode="drop")
-    )
-    arrived = lax.all_to_all(
-        buffer.reshape(expert_count, capacity, model_width),
-        "expert",
-        split_axis=0,
-        concat_axis=0,
-        tiled=True,
-    )
-    arrived = arrived.reshape(overflow, model_width)
+    arrived = exchange(buffer, 3)
     results = experts(arrived, w_in, b_in, w_out, b_out)
-    returned = lax.all_to_all(
-        results.reshape(expert_count, capacity, model_width),
-        "expert",
-        split_axis=0,
-        concat_axis=0,
-        tiled=True,
-    )
-    returned = returned.reshape(overflow, model_width)
-    gate_values = gate_code.astype(jnp.float32) / 65536.0
-    gate_flat = jnp.concatenate([gate_values[:, 0], gate_values[:, 1]])
-    weights = jnp.where(kept_mask, gate_flat, 0.0)
-    guard_index = jnp.minimum(slot_index, overflow - 1)
-    picked = returned[guard_index].astype(jnp.float32) * weights[:, None]
-    layer_out = hidden_state + picked[:tok_count] + picked[tok_count:]
-    return layer_out.astype(jnp.bfloat16)
+    returned = exchange(results, 4)
+    return combine(hidden_state, ids, gate_code, returned)
 
 
 def solution(mesh):

time: 205 us -> 172 us (0.84)
  the two profiles are of different devices: /device:TPU:8 before, /device:TPU:16 now
where the time goes in v2:
time: 172 us; the launch traced here: 171 us
  Pallas kernels  162 us (94%)
  local copies, waits for them, and re-layouts  8.6 us (5%)
    pallas_call x1, Pallas kernels, regroup_attend(): pl.pallas_call(regroup_kernel, out_shape=(jax.ShapeDtypeStruct((tokens, w...  64.5 us
    pallas_call x1, Pallas kernels, experts(): pl.pallas_call(expert_kernel, out_shape=jax.ShapeDtypeStruct((count, widt...  61.1 us
    pallas_call x2, Pallas kernels, exchange(): pl.pallas_call(exchange_kernel, out_shape=jax.ShapeDtypeStruct(shape, row...  34.1 us
    reshape x2, local copies, waits for them, and re-layouts, exchange(): rows.reshape(shape)  3.67 us

profile of v2, /device:TPU:16, one launch (start us, length us, event | category | flops | bytes accessed | tf_op | source)
XLA Modules:
  0.0 171.1 jit_solution(7574758779727357517)
XLA Ops:
  0.0 0.0 copy-start
  0.0 0.7 copy-done
  0.7 0.7 copy.15.gate_ref
  1.4 64.5 %regroup_attend.1 = (f32[128,2048]{1,0:T(8,128)}, bf16[64,2048]{1,0:T(8,128)(2,1)}) custom-call(s32[1,128]{1,0:T(1,128)} %bitcast.8, s32[1,128]{1,0:T(1,128)} %seg_ref.1, s32[2,128]{1,0:T(2,128)} %bitcast.6, f32[1,2048]{1,0:T(1,128)} %bitcast.4, f32[1,2048]{1,0:T(1,128)} %bitcast.5, bf16[128,2048]{1,0:T(8,128)(2,1)} %state_ref.1, ...), custom_call_target="tpu_custom_call" | custom-call | tf_op jit(solution)/shard_map/regroup_attend/pallas_call | solution.py:447
  65.9 1.8 %reshape.9.x_ref = bf16[32,2,2048]{2,1,0:T(2,128)(2,1)} reshape(bf16[64,2048]{1,0:T(8,128)(2,1)} %get-tuple-element.8) | data formatting | bytes 524288 | tf_op jit(solution)/shard_map/reshape | solution.py:524
  67.8 17.0 %exchange.2 = bf16[32,2,2048]{2,1,0:T(2,128)(2,1)} custom-call(bf16[32,2,2048]{2,1,0:T(2,128)(2,1)} %reshape.9.x_ref), custom_call_target="tpu_custom_call" | custom-call | tf_op jit(solution)/shard_map/exchange/pallas_call | solution.py:516
  84.8 1.8 %reshape_reshape.3.x_ref = bf16[2,32,2048]{2,1,0:T(8,128)(2,1)} reshape(bf16[32,2,2048]{2,1,0:T(2,128)(2,1)} %exchange.2) | data formatting | bytes 524288 | tf_op jit(solution)/shard_map/reshape;reshape | solution.py:219
  86.5 61.1 %expert_ring.1 = bf16[64,2048]{1,0:T(8,128)(2,1)} custom-call(bf16[2,32,2048]{2,1,0:T(8,128)(2,1)} %reshape_reshape.3.x_ref, bf16[1,2048,256]{2,1,0:T(8,128)(2,1)} %w1_ref.1, f32[1,256]{1,0:T(1,128)} %b1_ref.1, bf16[1,256,2048]{2,1,0:T(8,128)(2,1)} %w2_ref.1, f32[32,2048]{1,0:T(8,128)} %b2_ref.1), custom_call_target="tpu_custom_call" | custom-call | tf_op jit(solution)/shard_map/expert_ring/pallas_call | solution.py:194
  147.6 1.8 %reshape.10.x_ref = bf16[32,2,2048]{2,1,0:T(2,128)(2,1)} reshape(bf16[64,2048]{1,0:T(8,128)(2,1)} %expert_ring.1) | data formatting | bytes 524288 | tf_op jit(solution)/shard_map/reshape | solution.py:524
  149.4 17.1 %exchange.3 = bf16[32,2,2048]{2,1,0:T(2,128)(2,1)} custom-call(bf16[32,2,2048]{2,1,0:T(2,128)(2,1)} %reshape.10.x_ref), custom_call_target="tpu_custom_call" | custom-call | tf_op jit(solution)/shard_map/exchange/pallas_call | solution.py:516
  166.6 1.8 %reshape.11.rows_ref = bf16[64,2048]{1,0:T(8,128)(2,1)} reshape(bf16[32,2,2048]{2,1,0:T(2,128)(2,1)} %exchange.3) | data formatting | bytes 524288 | tf_op jit(solution)/shard_map/reshape | solution.py:525
  168.4 2.7 %combine.1 = bf16[128,2048]{1,0:T(8,128)(2,1)} custom-call(f32[128,2048]{1,0:T(8,128)} %get-tuple-element.7.hidden_ref, s32[2,128]{1,0:T(2,128)} %bitcast.7, s32[128,2]{1,0:T(8,128)} %copy.15.gate_ref, bf16[64,2048]{1,0:T(8,128)(2,1)} %reshape.11.rows_ref), custom_call_target="tpu_custom_call" | custom-call | tf_op jit(solution)/shard_map/combine/pallas_call | solution.py:544
Async XLA Ops:
  0.0 0.7 copy-start

commit v3 on v1

v3 whole, which is shorter than its diff:
```python
import math

import jax
import jax.numpy as jnp
from jax import lax
from jax.experimental import pallas as pl
from jax.experimental.pallas import tpu as pltpu
from jax.sharding import PartitionSpec as P

HEAD_DIM = 128
CAP = 2


epsilon = 1e-05
mask_fill = -1e30


MESH_ID = pl.DeviceIdType.MESH


F32 = jnp.float32
BF16 = jnp.bfloat16


def iota(shape, axis):
    return lax.broadcasted_iota(jnp.int32, shape, axis)


def as_column(row):
    count = row.shape[1]
    return jnp.transpose(jnp.broadcast_to(row, (count, count)))


def earlier_equal(row):
    count = row.shape[1]
    same = as_column(row) == jnp.broadcast_to(row, (count, count))
    before = iota((count, count), 0) < iota((count, count), 1)
    return jnp.sum((same & before).astype(F32), axis=0, keepdims=True)


def slot_row(ids_ref, expert_count):
    ids = ids_ref[...].astype(F32)
    assigned = jnp.concatenate([ids[0:1, :], ids[1:2, :]], axis=1)
    rank = earlier_equal(assigned)
    kept = (assigned < expert_count) & (rank < CAP)
    return jnp.where(kept, assigned * CAP + rank, -1.0)


def regroup_phase(
    pos_ref,
    seg_ref,
    gain_ref,
    bias_ref,
    state_ref,
    query_ref,
    key_ref,
    value_ref,
    hidden_ref,
    out_rows,
    in_rows,
    out_offs,
    in_offs,
    send_sem,
    recv_sem,
    await_barrier,
):
    peers = lax.axis_size("dp")
    me = lax.axis_index("dp")
    tokens, width = state_ref.shape
    per_target = tokens // peers
    chunks = out_rows.shape[0]
    part = width // chunks
    both = 2 * tokens

    pos = pos_ref[...]
    target = (pos // tokens).astype(F32)
    offset = (pos % tokens).astype(F32)
    place = target * (2 * per_target) + earlier_equal(target)
    places = jnp.concatenate([place, place + per_target], axis=1).astype(jnp.int32)
    spread = (iota((both, both), 0) == places).astype(F32).astype(BF16)
    offset_column = as_column(offset)
    offset_both = jnp.concatenate([offset_column, offset_column + tokens], axis=0).astype(BF16)
    out_offs[...] = (
        jnp.dot(spread, offset_both, preferred_element_type=F32)
        .astype(BF16)
        .reshape(peers, 2 * per_target, tokens)
    )

    def fill(c):
        cols = pl.ds(pl.multiple_of(c * part, part), part)
        upper = jnp.concatenate([state_ref[:, cols], query_ref[:, cols]], axis=1)
        lower = jnp.concatenate([key_ref[:, cols], value_ref[:, cols]], axis=1)
        joined = jnp.concatenate([upper, lower], axis=0)
        out_rows[c] = (
            jnp.dot(spread, joined, preferred_element_type=F32)
            .astype(BF16)
            .reshape(peers, 2 * per_target, 2 * part)
        )

    def send_rows(c, to, frm):
        return pltpu.make_async_remote_copy(
            src_ref=out_rows.at[c, to],
            dst_ref=in_rows.at[c, frm],
            send_sem=send_sem.at[c, to],
            recv_sem=recv_sem.at[c, frm],
            device_id={"dp": to},
            device_id_type=MESH_ID,
        )

    def send_offs(to, frm):
        return pltpu.make_async_remote_copy(
            src_ref=out_offs.at[to],
            dst_ref=in_offs.at[frm],
            send_sem=send_sem.at[chunks, to],
            recv_sem=recv_sem.at[chunks, frm],
            device_id={"dp": to},
            device_id_type=MESH_ID,
        )

    def own_rows(c):
        return pltpu.make_async_copy(out_rows.at[c, me], in_rows.at[c, me], recv_sem.at[c, me])

    own_offs = pltpu.make_async_copy(out_offs.at[me], in_offs.at[me], recv_sem.at[chunks, me])

    def order(k):
        step = (k + 1) // 2
        return (me + peers + step * (2 * (k % 2) - 1)) % peers

    fill(0)
    await_barrier()
    own_offs.start()

    def start_offs(k, carry):
        send_offs(order(k), me).start()
        return carry

    lax.fori_loop(1, peers, start_offs, 0)

    def start_chunk(c, carry):
        @pl.when(c > 0)
        def _():
            fill(c)

        own_rows(c).start()

        def start_rows(k, inner):
            send_rows(c, order(k), me).start()
            return inner

        return lax.fori_loop(1, peers, start_rows, carry)

    lax.fori_loop(0, chunks, start_chunk, 0)

    segs = seg_ref[...].astype(F32)
    same_doc = as_column(segs) == jnp.broadcast_to(segs, (tokens, tokens))

    own_offs.wait()

    def await_offs(k, carry):
        send_offs(me, (me + k) % peers).wait_recv()
        return carry

    lax.fori_loop(1, peers, await_offs, 0)
    offs = in_offs[...].reshape(both, tokens).astype(F32)
    lanes = iota((both, tokens), 1).astype(F32)
    gather = jnp.concatenate([offs == lanes, offs == lanes + tokens], axis=1).astype(F32)
    gather = jnp.transpose(gather).astype(BF16)
    score_scale = 1.0 / math.sqrt(HEAD_DIM)

    def attend(c, carry):
        own_rows(c).wait()

        def await_rows(k, inner):
            send_rows(c, me, (me + k) % peers).wait_recv()
            return inner

        lax.fori_loop(1, peers, await_rows, 0)
        packed = jnp.dot(
            gather, in_rows[c].reshape(both, 2 * part), preferred_element_type=F32
        )
        states = packed[:tokens, :part]
        query = packed[:tokens, part:].astype(BF16)
        key = packed[tokens:, :part].astype(BF16)
        value = packed[tokens:, part:].astype(BF16)
        for h in range(part // HEAD_DIM):
            cols = slice(h * HEAD_DIM, (h + 1) * HEAD_DIM)
            scores = lax.dot_general(
                query[:, cols],
                key[:, cols],
                (((1,), (1,)), ((), ())),
                preferred_element_type=F32,
            )
            scores = jnp.where(same_doc, scores * score_scale, mask_fill)
            terms = jnp.exp(scores - jnp.max(scores, axis=1, keepdims=True))
            probs = (terms / jnp.sum(terms, axis=1, keepdims=True)).astype(BF16)
            mixed = jnp.dot(probs, value[:, cols], preferred_element_type=F32)
            at = pl.ds(pl.multiple_of(c * part + h * HEAD_DIM, HEAD_DIM), HEAD_DIM)
            hidden_ref[:, at] = states[:, cols] + mixed
        return carry

    lax.fori_loop(0, chunks, attend, 0)
    hidden = hidden_ref[...]
    centered = hidden - jnp.mean(hidden, axis=1, keepdims=True)
    variance = jnp.mean(centered * centered, axis=1, keepdims=True)
    normed = centered * lax.rsqrt(variance + epsilon) * gain_ref[...] + bias_ref[...]
    def drain(k, carry):
        peer = (me + k) % peers
        send_offs(peer, me).wait_send()

        def drain_chunk(c, inner):
            send_rows(c, peer, me).wait_send()
            return inner

        return lax.fori_loop(0, chunks, drain_chunk, carry)

    return normed.astype(BF16), lambda: lax.fori_loop(1, peers, drain, 0)


def expert_phase(
    b1_ref,
    b2_ref,
    loads,
    rows,
    part,
    pair_in,
    run_out,
    run_in,
    w1_v,
    w2_v,
    ag_send,
    ag_recv,
    sib_send,
    sib_recv,
    pair_send,
    pair_recv,
    run_send,
    run_recv,
):
    chips = lax.axis_size("dp") // 2
    me = lax.axis_index("dp")
    z = me // 2
    core = me % 2
    ahead = ((z + 1) % chips) * 2 + core
    behind = ((z + chips - 1) % chips) * 2 + core
    sibling = z * 2 + 1 - core
    half, width = rows.shape[3], rows.shape[4]
    steps = chips

    def pass_on(s, way):
        return pltpu.make_async_remote_copy(
            src_ref=rows.at[s, 0, way],
            dst_ref=rows.at[s + 1, 0, way],
            send_sem=ag_send.at[s, way],
            recv_sem=ag_recv.at[s, way],
            device_id={"dp": (ahead, behind)[way]},
            device_id_type=MESH_ID,
        )

    def to_sibling(s):
        return pltpu.make_async_remote_copy(
            src_ref=rows.at[s, 0],
            dst_ref=rows.at[s, 1],
            send_sem=sib_send.at[s],
            recv_sem=sib_recv.at[s],
            device_id={"dp": sibling},
            device_id_type=MESH_ID,
        )

    def pair(s):
        return pltpu.make_async_remote_copy(
            src_ref=part.at[s, 1],
            dst_ref=pair_in.at[s],
            send_sem=pair_send.at[s],
            recv_sem=pair_recv.at[s],
            device_id={"dp": sibling},
            device_id_type=MESH_ID,
        )

    def run(s, way):
        return pltpu.make_async_remote_copy(
            src_ref=run_out.at[s - 1, way],
            dst_ref=run_in.at[s - 1, way],
            send_sem=run_send.at[s - 1, way],
            recv_sem=run_recv.at[s - 1, way],
            device_id={"dp": (ahead, behind)[way]},
            device_id_type=MESH_ID,
        )

    def step(i, carry):
        @pl.when(i < steps)
        def _():
            @pl.when(i >= 1)
            def _():
                for way in range(2):
                    pass_on(i - 1, way).wait_recv()

            @pl.when(i < steps - 1)
            def _():
                for way in range(2):
                    pass_on(i, way).start()

            to_sibling(i).start()

        @pl.when(i == 1)
        def _():
            for load in loads:
                load.wait()

        @pl.when((i >= 1) & (i <= steps))
        def _():
            s = i - 1
            to_sibling(s).wait_recv()
            held = rows[s].reshape(4 * half, width)
            hidden = jnp.dot(held, w1_v[...], preferred_element_type=jnp.float32)
            hidden = jnp.maximum(hidden + b1_ref[...], 0.0).astype(jnp.bfloat16)
            share = jnp.dot(hidden, w2_v[...], preferred_element_type=jnp.float32)
            part[s] = share.astype(jnp.bfloat16).reshape(2, 2, half, width)
            pair(s).start()

        @pl.when(i == 3)
        def _():
            pair(1).wait_recv()
            total = part[1, 0].astype(jnp.float32) + pair_in[1].astype(jnp.float32)
            run_out[0] = total.astype(jnp.bfloat16)
            for way in range(2):
                run(1, way).start()

        @pl.when(i > 3)
        def _():
            s = i - 2
            pair(s).wait_recv()
            total = part[s, 0].astype(jnp.float32) + pair_in[s].astype(jnp.float32)
            for way in range(2):
                run(s - 1, way).wait_recv()
            total = total + run_in[s - 2].astype(jnp.float32)
            run_out[s - 1] = total.astype(jnp.bfloat16)
            for way in range(2):
                run(s, way).start()

        return carry

    lax.fori_loop(0, steps + 2, step, 0)
    pair(0).wait_recv()
    total = part[0, 0].astype(jnp.float32) + pair_in[0].astype(jnp.float32)
    total = total + b2_ref[pl.ds(lax.axis_index("expert"), 1), :].reshape(1, 1, width)
    for way in range(2):
        run(steps - 1, way).wait_recv()
    total = total + run_in[steps - 2].astype(jnp.float32)
    results = total.reshape(2 * half, width)

    def drain(s, carry):
        to_sibling(s).wait_send()
        pair(s).wait_send()

        @pl.when(s < steps - 1)
        def _():
            for way in range(2):
                pass_on(s, way).wait_send()
                run(s + 1, way).wait_send()

        return carry

    return results, lambda: lax.fori_loop(0, steps, drain, 0)


def exchange_phase(out_ref, in_ref, send_sem, recv_sem):
    peers = lax.axis_size("expert")
    me = lax.axis_index("expert")
    own = pltpu.make_async_copy(out_ref.at[me], in_ref.at[me], recv_sem.at[me])

    def move(to, frm):
        return pltpu.make_async_remote_copy(
            src_ref=out_ref.at[to],
            dst_ref=in_ref.at[frm],
            send_sem=send_sem.at[to],
            recv_sem=recv_sem.at[frm],
            device_id={"expert": to},
            device_id_type=MESH_ID,
        )

    def start(k, carry):
        move((me + k) % peers, me).start()
        return carry

    lax.fori_loop(1, peers, start, 0)
    own.start()
    own.wait()

    def finish(k, carry):
        move(me, (me + k) % peers).wait_recv()
        return carry

    lax.fori_loop(1, peers, finish, 0)

    def drain(k, carry):
        move((me + k) % peers, me).wait_send()
        return carry

    return lambda: lax.fori_loop(1, peers, drain, 0)


def layer_kernel(
    pos_ref,
    seg_ref,
    ids_ref,
    gate_ref,
    gain_ref,
    bias_ref,
    state_ref,
    query_ref,
    key_ref,
    value_ref,
    w1_ref,
    b1_ref,
    w2_ref,
    b2_ref,
    o_ref,
    hidden_ref,
    out_rows,
    in_rows,
    out_offs,
    in_offs,
    send_sem,
    recv_sem,
    stage,
    out_msgs,
    in_msgs,
    back_out,
    back_in,
    msg_send,
    msg_recv,
    load_sem,
    rows,
    part,
    pair_in,
    run_out,
    run_in,
    w1_v,
    w2_v,
    *ring_sems,
):
    dp_count = lax.axis_size("dp")
    expert_count = lax.axis_size("expert")
    dp_me = lax.axis_index("dp")
    expert_me = lax.axis_index("expert")
    tokens, width = state_ref.shape
    count = expert_count * CAP
    piece = stage.shape[2]
    pieces = stage.shape[1]
    loads = (
        pltpu.make_async_copy(w1_ref.at[0], w1_v, load_sem.at[0]),
        pltpu.make_async_copy(w2_ref.at[0], w2_v, load_sem.at[1]),
    )
    barrier = pltpu.get_barrier_semaphore()

    def greet_expert(k, carry):
        peer = (expert_me + k) % expert_count
        pl.semaphore_signal(barrier, inc=1, device_id={"expert": peer}, device_id_type=MESH_ID)
        return carry

    def greet_dp(k, carry):
        peer = (dp_me + k) % dp_count
        pl.semaphore_signal(barrier, inc=1, device_id={"dp": peer}, device_id_type=MESH_ID)
        return carry

    lax.fori_loop(1, expert_count, greet_expert, 0)
    lax.fori_loop(1, dp_count, greet_dp, 0)
    for load in loads:
        load.start()

    normed, drain_rows = regroup_phase(
        pos_ref,
        seg_ref,
        gain_ref,
        bias_ref,
        state_ref,
        query_ref,
        key_ref,
        value_ref,
        hidden_ref,
        out_rows,
        in_rows,
        out_offs,
        in_offs,
        send_sem,
        recv_sem,
        lambda: pl.semaphore_wait(barrier, dp_count + expert_count - 2),
    )

    def pack(ref):
        ref[...] = stage[...].reshape(ref.shape[0] * ref.shape[1], piece).astype(BF16).reshape(ref.shape)

    def unpack(ref):
        stage[...] = ref[...].reshape(ref.shape[0] * ref.shape[1], piece).astype(F32).reshape(stage.shape)

    slots = slot_row(ids_ref, expert_count)
    slot_hot = (iota((count, 2 * tokens), 0) == slots.astype(jnp.int32)).astype(F32)
    slot_hot = (slot_hot[:, :tokens] + slot_hot[:, tokens:]).astype(BF16)
    buffer = jnp.dot(slot_hot, normed, preferred_element_type=F32)
    for b in range(pieces):
        stage[:, b, :] = buffer[:, b * piece : (b + 1) * piece]
    pack(out_msgs)
    drain_out = exchange_phase(out_msgs, in_msgs, msg_send.at[0], msg_recv.at[0])
    unpack(in_msgs)
    half = count // 2
    for b in range(pieces):
        rows[0, 0, :, :, b * piece : (b + 1) * piece] = (
            stage[:, b, :].astype(BF16).reshape(2, half, piece)
        )
    results, drain_ring = expert_phase(
        b1_ref, b2_ref, loads, rows, part, pair_in, run_out, run_in, w1_v, w2_v, *ring_sems
    )
    for b in range(pieces):
        stage[:, b, :] = results[:, b * piece : (b + 1) * piece]
    pack(back_out)
    drain_back = exchange_phase(back_out, back_in, msg_send.at[1], msg_recv.at[1])
    unpack(back_in)

    gates = gate_ref[...].astype(F32) / 65536.0
    hots, weights = [], []
    for choice in range(2):
        column = as_column(slots[:, choice * tokens : (choice + 1) * tokens])
        hot = (column == iota((tokens, tokens), 1).astype(F32)).astype(F32).astype(BF16)
        hots.append(hot[:, :count])
        weights.append(as_column(gates[choice : choice + 1, :])[:, 0:1])
    for b in range(pieces):
        cols = slice(b * piece, (b + 1) * piece)
        returned = stage[:, b, :].astype(BF16)
        total = hidden_ref[:, cols]
        for hot, weight in zip(hots, weights):
            total = total + jnp.dot(hot, returned, preferred_element_type=F32) * weight
        o_ref[:, cols] = total.astype(BF16)
    drain_rows()
    drain_out()
    drain_ring()
    drain_back()


def per_device(
    pivot_states,
    queries,
    keys,
    values,
    pack_pos,
    segment_ids,
    expert_ids,
    gate_code,
    ln_gain,
    ln_bias,
    w_in,
    b_in,
    w_out,
    b_out,
):
    tokens, width = pivot_states.shape
    units = w_in.shape[2]
    peers = lax.axis_size("dp")
    expert_count = lax.axis_size("expert")
    count = expert_count * CAP
    half = count // 2
    chips = peers // 2
    chunks = 4
    group = 2 * tokens // peers
    pieces = 8
    piece = width // pieces
    dma = pltpu.SemaphoreType.DMA
    vmem = pl.BlockSpec(memory_space=pltpu.VMEM)
    any_space = pl.BlockSpec(memory_space=pl.ANY)
    messages = pltpu.VMEM((expert_count, CAP * pieces, piece), BF16)
    return pl.pallas_call(
        layer_kernel,
        out_shape=jax.ShapeDtypeStruct((tokens, width), BF16),
        in_specs=[vmem] * 10 + [any_space, vmem, any_space, vmem],
        out_specs=vmem,
        scratch_shapes=[
            pltpu.VMEM((tokens, width), F32),
            pltpu.VMEM((chunks, peers, group, 2 * width // chunks), BF16),
            pltpu.VMEM((chunks, peers, group, 2 * width // chunks), BF16),
            pltpu.VMEM((peers, group, tokens), BF16),
            pltpu.VMEM((peers, group, tokens), BF16),
            dma((chunks + 1, peers)),
            dma((chunks + 1, peers)),
            pltpu.VMEM((count, pieces, piece), F32),
            messages,
            messages,
            messages,
            messages,
            dma((2, expert_count)),
            dma((2, expert_count)),
            dma((2,)),
            pltpu.VMEM((chips, 2, 2, half, width), BF16),
            pltpu.VMEM((chips, 2, 2, half, width), BF16),
            pltpu.VMEM((chips, 2, half, width), BF16),
            pltpu.VMEM((chips - 1, 2, half, width), BF16),
            pltpu.VMEM((chips - 1, 2, half, width), BF16),
            pltpu.VMEM((width, units), BF16),
            pltpu.VMEM((units, width), BF16),
            dma((chips - 1, 2)),
            dma((chips - 1, 2)),
            dma((chips,)),
            dma((chips,)),
            dma((chips,)),
            dma((chips,)),
            dma((chips - 1, 2)),
            dma((chips - 1, 2)),
        ],
        compiler_params=pltpu.CompilerParams(collective_id=1, has_side_effects=True),
        name="moe_layer",
    )(
        pack_pos[None, :],
        segment_ids,
        expert_ids.T,
        gate_code.T,
        ln_gain[None, :],
        ln_bias[None, :],
        pivot_states,
        queries,
        keys,
        values,
        w_in,
        b_in,
        w_out,
        b_out,
    )


def solution(mesh):
    return jax.shard_map(
        per_device,
        mesh=mesh,
        in_specs=(
            P(("dp", "expert"), None),
            P(("dp", "expert"), None),
            P(("dp", "expert"), None),
            P(("dp", "expert"), None),
            P(("dp", "expert")),
            P(("dp", "expert"), None),
            P(("dp", "expert"), None),
            P(("dp", "expert"), None),
            P(),
            P(),
            P("expert", None, "dp"),
            P("expert", "dp"),
            P("expert", "dp", None),
            P(),
        ),
        out_specs=P(("dp", "expert"), None),
        check_vma=False,
    )
```

time: 205 us -> 149 us (0.73)
  the two profiles are of different devices: /device:TPU:8 before, /device:TPU:2 now
where the time goes in v3:
time: 149 us
  Pallas kernels  147 us (99%)
  local copies, waits for them, and re-layouts  1.88 us (1%)
    pallas_call x1, Pallas kernels, per_device(): pl.pallas_call(layer_kernel, out_shape=jax.ShapeDtypeStruct((tokens, widt...  147 us

profile of v3, /device:TPU:2, one launch (start us, length us, event | category | flops | bytes accessed | tf_op | source)
XLA Modules:
  0.0 149.0 jit_solution(14656184536066295854)
XLA Ops:
  0.0 147.1 %moe_layer.1 = bf16[128,2048]{1,0:T(8,128)(2,1)} custom-call(s32[1,128]{1,0:T(1,128)} %bitcast.9, s32[1,128]{1,0:T(1,128)} %seg_ref.1, s32[2,128]{1,0:T(2,128)} %bitcast.7, s32[2,128]{1,0:T(2,128)} %bitcast.8, f32[1,2048]{1,0:T(1,128)} %bitcast.5, f32[1,2048]{1,0:T(1,128)} %bitcast.6, bf16[128,2048]{1,0:T(8,128)(2,1)} %state_ref.1, ...), custom_call_target="tpu_custom_call" | custom-call | tf_op jit(solution)/shard_map/moe_layer/pallas_call | solution.py:570
  147.2 1.9 %copy.16 = bf16[128,2048]{1,0:T(8,128)(2,1)} copy(bf16[128,2048]{1,0:T(8,128)(2,1)} %moe_layer.1) | data formatting | bytes 1048576

commit v4 on v3

--- a/solution.py
+++ b/solution.py
@@ -62,6 +62,9 @@
     in_offs,
     send_sem,
     recv_sem,
+    relay,
+    relay_recv,
+    relay_send,
     await_barrier,
 ):
     peers = lax.axis_size("dp")
@@ -122,34 +125,83 @@
 
     own_offs = pltpu.make_async_copy(out_offs.at[me], in_offs.at[me], recv_sem.at[chunks, me])
 
-    def order(k):
-        step = (k + 1) // 2
-        return (me + peers + step * (2 * (k % 2) - 1)) % peers
+    chips = peers // 2
+    z = me // 2
+    core = me % 2
+    opposite = chips // 2
+    hop = opposite // 2
+
+    def around(steps, on_core):
+        return ((z + chips + steps) % chips) * 2 + on_core
+
+    def to_relay(c, way):
+        to = around(opposite, (way + core) % 2)
+        return pltpu.make_async_remote_copy(
+            src_ref=out_rows.at[c, to],
+            dst_ref=relay.at[c, way],
+            send_sem=send_sem.at[c, to],
+            recv_sem=relay_recv.at[c, way],
+            device_id={"dp": around(hop * (1 - 2 * way), core)},
+            device_id_type=MESH_ID,
+        )
+
+    def forward(c, way):
+        frm = around(-hop * (1 - 2 * way), core)
+        return pltpu.make_async_remote_copy(
+            src_ref=relay.at[c, way],
+            dst_ref=in_rows.at[c, frm],
+            send_sem=relay_send.at[c, way],
+            recv_sem=recv_sem.at[c, frm],
+            device_id={"dp": around(hop * (1 - 2 * way), (way + core) % 2)},
+            device_id_type=MESH_ID,
+        )
+
+    def start_chunk(c, carry):
+        def start_rows(k, inner):
+            distance = opposite - 1 - k // 4
+            steps = distance * (1 - 2 * (k % 2))
+            send_rows(c, around(steps, (k // 2) % 2), me).start()
+            return inner
+
+        lax.fori_loop(0, 4 * (opposite - 1), start_rows, 0)
+        send_rows(c, around(0, 1 - core), me).start()
+        own_rows(c).start()
+        return carry
 
     fill(0)
     await_barrier()
     own_offs.start()
 
     def start_offs(k, carry):
-        send_offs(order(k), me).start()
+        send_offs((me + k) % peers, me).start()
         return carry
 
     lax.fori_loop(1, peers, start_offs, 0)
 
-    def start_chunk(c, carry):
+    def start_relays(c, carry):
         @pl.when(c > 0)
         def _():
             fill(c)
 
-        own_rows(c).start()
-
-        def start_rows(k, inner):
-            send_rows(c, order(k), me).start()
-            return inner
-
-        return lax.fori_loop(1, peers, start_rows, carry)
-
-    lax.fori_loop(0, chunks, start_chunk, 0)
+        for way in range(2):
+            to_relay(c, way).start()
+
+        @pl.when(c < ahead)
+        def _():
+            start_chunk(c, 0)
+
+        return carry
+
+    def pass_relays(c, carry):
+        for way in range(2):
+            to_relay(c, way).wait_recv()
+            forward(c, way).start()
+        return carry
+
+    ahead = chunks // 2
+    lax.fori_loop(0, chunks, start_relays, 0)
+    lax.fori_loop(0, chunks, pass_relays, 0)
+    lax.fori_loop(ahead, chunks, start_chunk, 0)
 
     segs = seg_ref[...].astype(F32)
     same_doc = as_column(segs) == jnp.broadcast_to(segs, (tokens, tokens))
@@ -213,7 +265,16 @@
 
         return lax.fori_loop(0, chunks, drain_chunk, carry)
 
-    return normed.astype(BF16), lambda: lax.fori_loop(1, peers, drain, 0)
+    def drain_relays(c, carry):
+        for way in range(2):
+            forward(c, way).wait_send()
+        return carry
+
+    def drain_all():
+        lax.fori_loop(1, peers, drain, 0)
+        lax.fori_loop(0, chunks, drain_relays, 0)
+
+    return normed.astype(BF16), drain_all
 
 
 def expert_phase(
@@ -422,6 +483,9 @@
     in_offs,
     send_sem,
     recv_sem,
+    relay,
+    relay_recv,
+    relay_send,
     stage,
     out_msgs,
     in_msgs,
@@ -484,6 +548,9 @@
         in_offs,
         send_sem,
         recv_sem,
+        relay,
+        relay_recv,
+        relay_send,
         lambda: pl.semaphore_wait(barrier, dp_count + expert_count - 2),
     )
 
@@ -580,6 +647,9 @@
             pltpu.VMEM((peers, group, tokens), BF16),
             dma((chunks + 1, peers)),
             dma((chunks + 1, peers)),
+            pltpu.VMEM((chunks, 2, group, 2 * width // chunks), BF16),
+            dma((chunks, 2)),
+            dma((chunks, 2)),
             pltpu.VMEM((count, pieces, piece), F32),
             messages,
             messages,

time: 149 us -> 149 us (level)
  no operation moved by 1% of the time
where the time goes in v4:
time: 149 us
  Pallas kernels  147 us (99%)
  local copies, waits for them, and re-layouts  1.88 us (1%)
    pallas_call x1, Pallas kernels, per_device(): pl.pallas_call(layer_kernel, out_shape=jax.ShapeDtypeStruct((tokens, widt...  147 us

profile of v4, /device:TPU:2, one launch (start us, length us, event | category | flops | bytes accessed | tf_op | source)
XLA Modules:
  0.0 148.8 jit_solution(12368806154603224086)
XLA Ops:
  0.0 146.9 %moe_layer.1 = bf16[128,2048]{1,0:T(8,128)(2,1)} custom-call(s32[1,128]{1,0:T(1,128)} %bitcast.9, s32[1,128]{1,0:T(1,128)} %seg_ref.1, s32[2,128]{1,0:T(2,128)} %bitcast.7, s32[2,128]{1,0:T(2,128)} %bitcast.8, f32[1,2048]{1,0:T(1,128)} %bitcast.5, f32[1,2048]{1,0:T(1,128)} %bitcast.6, bf16[128,2048]{1,0:T(8,128)(2,1)} %state_ref.1, ...), custom_call_target="tpu_custom_call" | custom-call | tf_op jit(solution)/shard_map/moe_layer/pallas_call | solution.py:637
  146.9 1.9 %copy.16 = bf16[128,2048]{1,0:T(8,128)(2,1)} copy(bf16[128,2048]{1,0:T(8,128)(2,1)} %moe_layer.1) | data formatting | bytes 1048576

commit v5 on v4

--- a/solution.py
+++ b/solution.py
@@ -307,12 +307,16 @@
     half, width = rows.shape[3], rows.shape[4]
     steps = chips
 
-    def pass_on(s, way):
-        return pltpu.make_async_remote_copy(
-            src_ref=rows.at[s, 0, way],
-            dst_ref=rows.at[s + 1, 0, way],
-            send_sem=ag_send.at[s, way],
-            recv_sem=ag_recv.at[s, way],
+    quarter = half // 2
+    lanes = [(way, sub) for sub in range(2) for way in range(2)]
+
+    def pass_on(s, way, sub):
+        at = pl.ds(sub * quarter, quarter)
+        return pltpu.make_async_remote_copy(
+            src_ref=rows.at[s, 0, way, at],
+            dst_ref=rows.at[s + 1, 0, way, at],
+            send_sem=ag_send.at[s, way, sub],
+            recv_sem=ag_recv.at[s, way, sub],
             device_id={"dp": (ahead, behind)[way]},
             device_id_type=MESH_ID,
         )
@@ -337,12 +341,13 @@
             device_id_type=MESH_ID,
         )
 
-    def run(s, way):
-        return pltpu.make_async_remote_copy(
-            src_ref=run_out.at[s - 1, way],
-            dst_ref=run_in.at[s - 1, way],
-            send_sem=run_send.at[s - 1, way],
-            recv_sem=run_recv.at[s - 1, way],
+    def run(s, way, sub):
+        at = pl.ds(sub * quarter, quarter)
+        return pltpu.make_async_remote_copy(
+            src_ref=run_out.at[s - 1, way, at],
+            dst_ref=run_in.at[s - 1, way, at],
+            send_sem=run_send.at[s - 1, way, sub],
+            recv_sem=run_recv.at[s - 1, way, sub],
             device_id={"dp": (ahead, behind)[way]},
             device_id_type=MESH_ID,
         )
@@ -350,15 +355,15 @@
     def step(i, carry):
         @pl.when(i < steps)
         def _():
-            @pl.when(i >= 1)
-            def _():
-                for way in range(2):
-                    pass_on(i - 1, way).wait_recv()
-
-            @pl.when(i < steps - 1)
-            def _():
-                for way in range(2):
-                    pass_on(i, way).start()
+            for way, sub in lanes:
+
+                @pl.when(i >= 1)
+                def _():
+                    pass_on(i - 1, way, sub).wait_recv()
+
+                @pl.when(i < steps - 1)
+                def _():
+                    pass_on(i, way, sub).start()
 
             to_sibling(i).start()
 
@@ -383,20 +388,21 @@
             pair(1).wait_recv()
             total = part[1, 0].astype(jnp.float32) + pair_in[1].astype(jnp.float32)
             run_out[0] = total.astype(jnp.bfloat16)
-            for way in range(2):
-                run(1, way).start()
+            for way, sub in lanes:
+                run(1, way, sub).start()
 
         @pl.when(i > 3)
         def _():
             s = i - 2
             pair(s).wait_recv()
-            total = part[s, 0].astype(jnp.float32) + pair_in[s].astype(jnp.float32)
-            for way in range(2):
-                run(s - 1, way).wait_recv()
-            total = total + run_in[s - 2].astype(jnp.float32)
-            run_out[s - 1] = total.astype(jnp.bfloat16)
-            for way in range(2):
-                run(s, way).start()
+            for way, sub in lanes:
+                at = slice(sub * quarter, (sub + 1) * quarter)
+                total = part[s, 0, way, at].astype(jnp.float32)
+                total = total + pair_in[s, way, at].astype(jnp.float32)
+                run(s - 1, way, sub).wait_recv()
+                total = total + run_in[s - 2, way, at].astype(jnp.float32)
+                run_out[s - 1, way, at] = total.astype(jnp.bfloat16)
+                run(s, way, sub).start()
 
         return carry
 
@@ -404,8 +410,8 @@
     pair(0).wait_recv()
     total = part[0, 0].astype(jnp.float32) + pair_in[0].astype(jnp.float32)
     total = total + b2_ref[pl.ds(lax.axis_index("expert"), 1), :].reshape(1, 1, width)
-    for way in range(2):
-        run(steps - 1, way).wait_recv()
+    for way, sub in lanes:
+        run(steps - 1, way, sub).wait_recv()
     total = total + run_in[steps - 2].astype(jnp.float32)
     results = total.reshape(2 * half, width)
 
@@ -415,9 +421,9 @@
 
         @pl.when(s < steps - 1)
         def _():
-            for way in range(2):
-                pass_on(s, way).wait_send()
-                run(s + 1, way).wait_send()
+            for way, sub in lanes:
+                pass_on(s, way, sub).wait_send()
+                run(s + 1, way, sub).wait_send()
 
         return carry
 
@@ -665,14 +671,14 @@
             pltpu.VMEM((chips - 1, 2, half, width), BF16),
             pltpu.VMEM((width, units), BF16),
             pltpu.VMEM((units, width), BF16),
-            dma((chips - 1, 2)),
-            dma((chips - 1, 2)),
+            dma((chips - 1, 2, 2)),
+            dma((chips - 1, 2, 2)),
             dma((chips,)),
             dma((chips,)),
             dma((chips,)),
             dma((chips,)),
-            dma((chips - 1, 2)),
-            dma((chips - 1, 2)),
+            dma((chips - 1, 2, 2)),
+            dma((chips - 1, 2, 2)),
         ],
         compiler_params=pltpu.CompilerParams(collective_id=1, has_side_effects=True),
         name="moe_layer",

time: 149 us -> 143 us (0.960)
  Pallas kernels: 147 us -> 141 us
    pallas_call x1, Pallas kernels: 147 us -> 141 us  [per_device(): pl.pallas_call(layer_kernel, out_shape=jax.ShapeDtypeStruct((tokens, widt...]
where the time goes in v5:
time: 143 us
  Pallas kernels  141 us (99%)
  local copies, waits for them, and re-layouts  1.88 us (1%)
    pallas_call x1, Pallas kernels, per_device(): pl.pallas_call(layer_kernel, out_shape=jax.ShapeDtypeStruct((tokens, widt...  141 us

profile of v5, /device:TPU:2, one launch (start us, length us, event | category | flops | bytes accessed | tf_op | source)
XLA Modules:
  0.0 142.8 jit_solution(14825521988932666146)
XLA Ops:
  0.0 140.9 %moe_layer.1 = bf16[128,2048]{1,0:T(8,128)(2,1)} custom-call(s32[1,128]{1,0:T(1,128)} %bitcast.9, s32[1,128]{1,0:T(1,128)} %seg_ref.1, s32[2,128]{1,0:T(2,128)} %bitcast.7, s32[2,128]{1,0:T(2,128)} %bitcast.8, f32[1,2048]{1,0:T(1,128)} %bitcast.5, f32[1,2048]{1,0:T(1,128)} %bitcast.6, bf16[128,2048]{1,0:T(8,128)(2,1)} %state_ref.1, ...), custom_call_target="tpu_custom_call" | custom-call | tf_op jit(solution)/shard_map/moe_layer/pallas_call | solution.py:643
  140.9 1.9 %copy.16 = bf16[128,2048]{1,0:T(8,128)(2,1)} copy(bf16[128,2048]{1,0:T(8,128)(2,1)} %moe_layer.1) | data formatting | bytes 1048576
